TPU v7x, 128 devices: a whole 4x4x4 slice. The times are simulated.
128 devices in a mesh: ctx: 16 (over x, y), tp: 8 (over z, core).
Axes of the slice: x: 4, y: 4, z: 4, core: 2. Of those that a mesh axis runs over, the one named last changes fastest.
Arguments:
- main_q: bfloat16 [7168, 24576], P('ctx', 'tp'), may hold values from -6 to 6
- main_k: bfloat16 [2048, 24576], P('ctx', 'tp'), may hold values from -6 to 6
- log_norms: float32 [7168, 128], P('ctx', 'tp'), may hold values from 0 to 4
- index_q: bfloat16 [7168, 64, 128], P(('ctx', 'tp')), may hold values from -8 to 8
- index_w: float32 [7168, 64], P(('ctx', 'tp')), may hold values from -2 to 2
- index_k: bfloat16 [2048, 128], P('ctx'), may hold values from -8 to 8
- row_weight: float32 [7168], P(('ctx', 'tp')), may hold values from 10 to 200
- offsets: int32 [16], P('ctx'), may hold values from 0 to 1600
- key_map: int32 [16], replicated, may hold values from 0 to 15, as said below
Outputs:
- grad_index_q: float32 [7168, 64, 128], P(('ctx', 'tp'))
- grad_index_w: float32 [7168, 64], P(('ctx', 'tp'))
- grad_index_k: float32 [2048, 128], P(('ctx', 'tp'))
Inputs may be any that keep to these rules, and one draw needn't show every extreme that they name: `key_map`: each key block number appears exactly once.
All inputs are finite; a program needn't handle non-finite values.
Results may differ from a plain program's by a relative error of at most 0.0028.
Values may be sent and summed in bfloat16 or wider, within the bound.
A program may use at most 128 MiB of HBM per device.

v0:
```python
import math

import jax
import jax.numpy as jnp
from jax import lax
from jax.sharding import PartitionSpec as P


def in_one_piece(arrays, axis, dim, along):
    both = jnp.concatenate(arrays, axis=along)
    out, at, done = (lax.all_gather(both, axis, axis=dim, tiled=True), 0, [])
    for a in arrays:
        done.append(lax.slice_in_dim(out, at, at + a.shape[along], axis=along))
        at += a.shape[along]
    return tuple(done)


def cut_along(array, dim, length):
    shape = array.shape
    parts = array.reshape(*shape[:dim], length, shape[dim] // length, *shape[dim + 1 :])
    return jnp.moveaxis(parts, dim, 0)


def summed_on_arrival(array, axis, dim):
    length = lax.axis_size(axis)
    parts = lax.all_to_all(cut_along(array, dim, length), axis, 0, 0, tiled=True)
    return jnp.sum(parts, axis=0)


def key_places(key_map, key_total, key_rows):
    storage = jnp.arange(key_total, dtype=jnp.int32)
    owners = storage // key_rows
    block_ids = jnp.arange(key_map.shape[0], dtype=jnp.int32)
    picked = jnp.sum(jnp.where(owners[:, None] == block_ids[None, :], key_map[None, :], 0), axis=1)
    return picked * key_rows + storage % key_rows


def column_mass(queries, norm_rows, row_pos, keys, key_pos):
    amount = queries.shape[0]
    heads = norm_rows.shape[1]
    key_total = keys.shape[0]
    block_keys = math.gcd(key_total, 256)
    queries_wide = queries.reshape(amount, heads, -1)
    score_scale = 1.0 / math.sqrt(queries_wide.shape[2])

    def add_block(number, running):
        first_key = number * block_keys
        key_block = lax.dynamic_slice_in_dim(keys, first_key, block_keys, 0).reshape(
            block_keys, heads, -1
        )
        key_place = lax.dynamic_slice_in_dim(key_pos, first_key, block_keys, 0)
        scores = (
            jnp.einsum("qhd,khd->qhk", queries_wide, key_block, preferred_element_type=jnp.float32)
            * score_scale
        )
        visible = key_place[None, :] <= row_pos[:, None]
        prob_terms = jnp.where(visible[:, None, :], jnp.exp(scores - norm_rows[:, :, None]), 0.0)
        return lax.dynamic_update_slice_in_dim(running, jnp.sum(prob_terms, axis=1), first_key, 1)

    return lax.fori_loop(
        0, key_total // block_keys, add_block, jnp.zeros((amount, key_total), jnp.float32)
    )


def per_device(main_q, main_k, log_norms, index_q, index_w, index_k, row_weight, offsets, key_map):
    key_rows = main_k.shape[0]
    block_rows = main_q.shape[0]
    own_rows = index_q.shape[0]
    key_total = key_rows * lax.axis_size("ctx")
    key_pos = key_places(key_map, key_total, key_rows)
    first_pos = offsets[0]
    block_pos = first_pos + jnp.arange(block_rows, dtype=jnp.int32)
    pieces = in_one_piece((main_k, index_k), "ctx", 0, 1)
    partial_mass = column_mass(main_q, log_norms, block_pos, pieces[0], key_pos)
    index_keys = pieces[1]
    row_mass = lax.psum_scatter(partial_mass, "tp", scatter_dimension=0, tiled=True)
    target = row_mass / jnp.sum(row_mass, axis=1, keepdims=True)
    own_pos = first_pos + lax.axis_index("tp") * own_rows + jnp.arange(own_rows, dtype=jnp.int32)
    visible = key_pos[None, :] <= own_pos[:, None]
    inv_root = 1.0 / math.sqrt(index_q.shape[2])
    block_keys = math.gcd(key_total, 256)
    block_count = key_total // block_keys

    def raw_scores(number):
        key_block = lax.dynamic_slice_in_dim(index_keys, number * block_keys, block_keys, 0)
        inner = (
            jnp.einsum("tjd,kd->tjk", index_q, key_block, preferred_element_type=jnp.float32)
            * inv_root
        )
        return (key_block, inner)

    def first_pass(number, logits):
        key_block, inner = raw_scores(number)
        part_logits = jnp.sum(index_w[:, :, None] * jax.nn.softplus(inner), axis=1)
        return lax.dynamic_update_slice_in_dim(logits, part_logits, number * block_keys, 1)

    logits = lax.fori_loop(
        0, block_count, first_pass, jnp.zeros((own_rows, key_total), jnp.float32)
    )
    masked = jnp.where(visible, logits, -jnp.inf)
    row_max = jnp.max(masked, axis=1, keepdims=True)
    exp_terms = jnp.exp(masked - row_max)
    index_probs = exp_terms / jnp.sum(exp_terms, axis=1, keepdims=True)
    logit_grad = row_weight[:, None] * (index_probs - target)

    def second_pass(number, running):
        grad_w, grad_q, key_terms = running
        key_block, inner = raw_scores(number)
        first_key = number * block_keys
        grad_part = lax.dynamic_slice_in_dim(logit_grad, first_key, block_keys, 1)
        grad_w = grad_w + jnp.sum(grad_part[:, None, :] * jax.nn.softplus(inner), axis=2)
        score_grad = (
            grad_part[:, None, :] * index_w[:, :, None] * jax.nn.sigmoid(inner) * inv_root
        ).astype(jnp.bfloat16)
        grad_q = grad_q + jnp.einsum(
            "tjk,kd->tjd", score_grad, key_block, preferred_element_type=jnp.float32
        )
        key_part = jnp.einsum(
            "tjk,tjd->kd", score_grad, index_q, preferred_element_type=jnp.float32
        )
        key_terms = lax.dynamic_update_slice_in_dim(key_terms, key_part, first_key, 0)
        return (grad_w, grad_q, key_terms)

    start_state = (
        jnp.zeros(index_w.shape, jnp.float32),
        jnp.zeros(index_q.shape, jnp.float32),
        jnp.zeros((key_total, index_q.shape[2]), jnp.float32),
    )
    grad_w, grad_q, key_terms = lax.fori_loop(0, block_count, second_pass, start_state)
    ctx_sums = summed_on_arrival(key_terms, "ctx", 0)
    grad_k = summed_on_arrival(ctx_sums, "tp", 0)
    return (grad_q, grad_w, grad_k)


def solution(mesh):
    placed = (
        P("ctx", "tp"),
        P("ctx", "tp"),
        P("ctx", "tp"),
        P(("ctx", "tp"), None, None),
        P(("ctx", "tp"), None),
        P("ctx", None),
        P(("ctx", "tp")),
        P("ctx"),
        P(),
    )
    return jax.shard_map(
        per_device,
        mesh=mesh,
        in_specs=placed,
        out_specs=(P(("ctx", "tp"), None, None), P(("ctx", "tp"), None), P(("ctx", "tp"), None)),
        check_vma=False,
    )
```

profile of v0, /device:TPU:1, one launch (start us, length us, event | category | flops | bytes accessed | tf_op | source)
XLA Modules:
  0.0 342.1 jit_solution(4529713366238152070)
XLA Ops:
  7.2 2.1 pad_maximum_fusion
  9.4 4.6 %copy.14 = bf16[448,3072]{0,1:T(8,128)(2,1)} copy(bf16[448,3072]{1,0:T(8,128)(2,1)} %param.15) | data formatting | bytes 5505024 | tf_op args[0]
  14.1 92.0 %all-gather.2.cloned.1.call-done = bf16[2048,3200]{1,0:T(8,128)(2,1)} async-done(((bf16[128,3200]{1,0:T(8,128)(2,1)}), bf16[2048,3200]{1,0:T(8,128)(2,1)}) %all-gather.2.cloned.1.call-update) | async-done | bytes 13107216 | tf_op jit(solution)/shard_map/all_gather | solution.py:11
  106.1 10.7 %slice.9 = bf16[2048,3072]{1,0:T(8,128)(2,1)} slice(bf16[2048,3200]{1,0:T(8,128)(2,1)} %all-gather.2.cloned.1.call-done), slice={[0:2048], [0:3072]} | slice | bytes 25165824 | tf_op jit(solution)/shard_map/slice | solution.py:13
  116.8 2.2 broadcast_in_dim.95
  119.0 68.4 %while.46 = (s32[]{:T(128)}, f32[448,2048]{1,0:T(8,128)}, s32[2048]{0:T(1024)S(1)}, bf16[2048,3072]{1,0:T(8,128)(2,1)}, bf16[448,16,192]{0,2,1:T(8,128)(2,1)}, /...) while((s32[]{:T(128)}, f32[448,2048]{1,0:T(8,128)}, ...), condition=%wide.region_8.9_spmd.clone, body=%wide.region_6.8_spmd.clone.sunk | while | flops 711983552 | bytes 12257963 | solution.py:60
  119.9 1.5 constant_dynamic-slice_fusion.4
  122.1 4.6 %fusion.69 = f32[448,256]{1,0:T(8,128)S(1)} fusion(f32[448,16]{0,1:T(8,128)S(1)} %get-tuple-element.621, pred[448,256]{1,0:T(8,128)(4,1)S(1)} %broadcast_compare_fusion.2, bf16[256,16,192]{0,2,1:T(8,128)(2,1)S(1)} %bitcast.110, bf16[448,16,192]{0,2,1:T(8,128)(2,1)} %get-tuple-element.620), kind=kOutput, calls=%fused_computation.17.clone.1 | convolution fusion | flops 711868416 | bytes 4927488 | tf_op jit(solution)/shard_map/while/body/eval_jaxpr/qhd,khd->qhk/dot_general | solution.py:53
  128.4 1.5 constant_dynamic-slice_fusion.4
  130.7 4.6 %fusion.69 = f32[448,256]{1,0:T(8,128)S(1)} fusion(f32[448,16]{0,1:T(8,128)S(1)} %get-tuple-element.621, pred[448,256]{1,0:T(8,128)(4,1)S(1)} %broadcast_compare_fusion.2, bf16[256,16,192]{0,2,1:T(8,128)(2,1)S(1)} %bitcast.110, bf16[448,16,192]{0,2,1:T(8,128)(2,1)} %get-tuple-element.620), kind=kOutput, calls=%fused_computation.17.clone.1 | convolution fusion | flops 711868416 | bytes 4927488 | tf_op jit(solution)/shard_map/while/body/eval_jaxpr/qhd,khd->qhk/dot_general | solution.py:53
  137.0 1.5 constant_dynamic-slice_fusion.4
  139.2 4.6 %fusion.69 = f32[448,256]{1,0:T(8,128)S(1)} fusion(f32[448,16]{0,1:T(8,128)S(1)} %get-tuple-element.621, pred[448,256]{1,0:T(8,128)(4,1)S(1)} %broadcast_compare_fusion.2, bf16[256,16,192]{0,2,1:T(8,128)(2,1)S(1)} %bitcast.110, bf16[448,16,192]{0,2,1:T(8,128)(2,1)} %get-tuple-element.620), kind=kOutput, calls=%fused_computation.17.clone.1 | convolution fusion | flops 711868416 | bytes 4927488 | tf_op jit(solution)/shard_map/while/body/eval_jaxpr/qhd,khd->qhk/dot_general | solution.py:53
  145.6 1.5 constant_dynamic-slice_fusion.4
  147.8 4.6 %fusion.69 = f32[448,256]{1,0:T(8,128)S(1)} fusion(f32[448,16]{0,1:T(8,128)S(1)} %get-tuple-element.621, pred[448,256]{1,0:T(8,128)(4,1)S(1)} %broadcast_compare_fusion.2, bf16[256,16,192]{0,2,1:T(8,128)(2,1)S(1)} %bitcast.110, bf16[448,16,192]{0,2,1:T(8,128)(2,1)} %get-tuple-element.620), kind=kOutput, calls=%fused_computation.17.clone.1 | convolution fusion | flops 711868416 | bytes 4927488 | tf_op jit(solution)/shard_map/while/body/eval_jaxpr/qhd,khd->qhk/dot_general | solution.py:53
  154.1 1.5 constant_dynamic-slice_fusion.4
  156.3 4.6 %fusion.69 = f32[448,256]{1,0:T(8,128)S(1)} fusion(f32[448,16]{0,1:T(8,128)S(1)} %get-tuple-element.621, pred[448,256]{1,0:T(8,128)(4,1)S(1)} %broadcast_compare_fusion.2, bf16[256,16,192]{0,2,1:T(8,128)(2,1)S(1)} %bitcast.110, bf16[448,16,192]{0,2,1:T(8,128)(2,1)} %get-tuple-element.620), kind=kOutput, calls=%fused_computation.17.clone.1 | convolution fusion | flops 711868416 | bytes 4927488 | tf_op jit(solution)/shard_map/while/body/eval_jaxpr/qhd,khd->qhk/dot_general | solution.py:53
  164.9 4.6 %fusion.69 = f32[448,256]{1,0:T(8,128)S(1)} fusion(f32[448,16]{0,1:T(8,128)S(1)} %get-tuple-element.621, pred[448,256]{1,0:T(8,128)(4,1)S(1)} %broadcast_compare_fusion.2, bf16[256,16,192]{0,2,1:T(8,128)(2,1)S(1)} %bitcast.110, bf16[448,16,192]{0,2,1:T(8,128)(2,1)} %get-tuple-element.620), kind=kOutput, calls=%fused_computation.17.clone.1 | convolution fusion | flops 711868416 | bytes 4927488 | tf_op jit(solution)/shard_map/while/body/eval_jaxpr/qhd,khd->qhk/dot_general | solution.py:53
  173.4 4.6 %fusion.69 = f32[448,256]{1,0:T(8,128)S(1)} fusion(f32[448,16]{0,1:T(8,128)S(1)} %get-tuple-element.621, pred[448,256]{1,0:T(8,128)(4,1)S(1)} %broadcast_compare_fusion.2, bf16[256,16,192]{0,2,1:T(8,128)(2,1)S(1)} %bitcast.110, bf16[448,16,192]{0,2,1:T(8,128)(2,1)} %get-tuple-element.620), kind=kOutput, calls=%fused_computation.17.clone.1 | convolution fusion | flops 711868416 | bytes 4927488 | tf_op jit(solution)/shard_map/while/body/eval_jaxpr/qhd,khd->qhk/dot_general | solution.py:53
  181.9 4.6 %fusion.69 = f32[448,256]{1,0:T(8,128)S(1)} fusion(f32[448,16]{0,1:T(8,128)S(1)} %get-tuple-element.621, pred[448,256]{1,0:T(8,128)(4,1)S(1)} %broadcast_compare_fusion.2, bf16[256,16,192]{0,2,1:T(8,128)(2,1)S(1)} %bitcast.110, bf16[448,16,192]{0,2,1:T(8,128)(2,1)} %get-tuple-element.620), kind=kOutput, calls=%fused_computation.17.clone.1 | convolution fusion | flops 711868416 | bytes 4927488 | tf_op jit(solution)/shard_map/while/body/eval_jaxpr/qhd,khd->qhk/dot_general | solution.py:53
  188.5 33.0 %while.45 = (s32[]{:T(128)}, f32[56,2048]{1,0:T(8,128)S(1)}, f32[56,64]{1,0:T(8,128)S(1)}, bf16[2048,128]{1,0:T(8,128)(2,1)S(1)}, bf16[56,64,128]{2,1,0:T(8,128)...) while((s32[]{:T(128)}, f32[56,2048]{1,0:T(8,128)S(1)}, f32[56,64]{1,0:T(8,128)S(1)}, ...), condition=%wide.region_3.4_spmd, body=%wide.region_1.3_spmd.sunk | while | flops 243124224 | bytes 1183891 | solution.py:97
  188.5 4.1 %fusion.66 = f32[56,256]{1,0:T(8,128)S(1)} fusion(bf16[56,64,128]{2,1,0:T(8,128)(2,1)} %get-tuple-element.649, f32[56,64]{1,0:T(8,128)S(1)} %get-tuple-element.647, bf16[2048,128]{1,0:T(8,128)(2,1)S(1)} %get-tuple-element.648, s32[]{:T(128)S(6)} %select_n.118), kind=kOutput, calls=%fused_computation.3.clone.1 | convolution fusion | flops 243124224 | bytes 1069060 | tf_op jit(solution)/shard_map/while/body/eval_jaxpr/tjd,kd->tjk/dot_general | solution.py:87
  192.6 4.1 %fusion.66 = f32[56,256]{1,0:T(8,128)S(1)} fusion(bf16[56,64,128]{2,1,0:T(8,128)(2,1)} %get-tuple-element.649, f32[56,64]{1,0:T(8,128)S(1)} %get-tuple-element.647, bf16[2048,128]{1,0:T(8,128)(2,1)S(1)} %get-tuple-element.648, s32[]{:T(128)S(6)} %select_n.118), kind=kOutput, calls=%fused_computation.3.clone.1 | convolution fusion | flops 243124224 | bytes 1069060 | tf_op jit(solution)/shard_map/while/body/eval_jaxpr/tjd,kd->tjk/dot_general | solution.py:87
  196.7 4.1 %fusion.66 = f32[56,256]{1,0:T(8,128)S(1)} fusion(bf16[56,64,128]{2,1,0:T(8,128)(2,1)} %get-tuple-element.649, f32[56,64]{1,0:T(8,128)S(1)} %get-tuple-element.647, bf16[2048,128]{1,0:T(8,128)(2,1)S(1)} %get-tuple-element.648, s32[]{:T(128)S(6)} %select_n.118), kind=kOutput, calls=%fused_computation.3.clone.1 | convolution fusion | flops 243124224 | bytes 1069060 | tf_op jit(solution)/shard_map/while/body/eval_jaxpr/tjd,kd->tjk/dot_general | solution.py:87
  200.8 4.1 %fusion.66 = f32[56,256]{1,0:T(8,128)S(1)} fusion(bf16[56,64,128]{2,1,0:T(8,128)(2,1)} %get-tuple-element.649, f32[56,64]{1,0:T(8,128)S(1)} %get-tuple-element.647, bf16[2048,128]{1,0:T(8,128)(2,1)S(1)} %get-tuple-element.648, s32[]{:T(128)S(6)} %select_n.118), kind=kOutput, calls=%fused_computation.3.clone.1 | convolution fusion | flops 243124224 | bytes 1069060 | tf_op jit(solution)/shard_map/while/body/eval_jaxpr/tjd,kd->tjk/dot_general | solution.py:87
  205.0 4.1 %fusion.66 = f32[56,256]{1,0:T(8,128)S(1)} fusion(bf16[56,64,128]{2,1,0:T(8,128)(2,1)} %get-tuple-element.649, f32[56,64]{1,0:T(8,128)S(1)} %get-tuple-element.647, bf16[2048,128]{1,0:T(8,128)(2,1)S(1)} %get-tuple-element.648, s32[]{:T(128)S(6)} %select_n.118), kind=kOutput, calls=%fused_computation.3.clone.1 | convolution fusion | flops 243124224 | bytes 1069060 | tf_op jit(solution)/shard_map/while/body/eval_jaxpr/tjd,kd->tjk/dot_general | solution.py:87
  209.1 4.1 %fusion.66 = f32[56,256]{1,0:T(8,128)S(1)} fusion(bf16[56,64,128]{2,1,0:T(8,128)(2,1)} %get-tuple-element.649, f32[56,64]{1,0:T(8,128)S(1)} %get-tuple-element.647, bf16[2048,128]{1,0:T(8,128)(2,1)S(1)} %get-tuple-element.648, s32[]{:T(128)S(6)} %select_n.118), kind=kOutput, calls=%fused_computation.3.clone.1 | convolution fusion | flops 243124224 | bytes 1069060 | tf_op jit(solution)/shard_map/while/body/eval_jaxpr/tjd,kd->tjk/dot_general | solution.py:87
  213.2 4.1 %fusion.66 = f32[56,256]{1,0:T(8,128)S(1)} fusion(bf16[56,64,128]{2,1,0:T(8,128)(2,1)} %get-tuple-element.649, f32[56,64]{1,0:T(8,128)S(1)} %get-tuple-element.647, bf16[2048,128]{1,0:T(8,128)(2,1)S(1)} %get-tuple-element.648, s32[]{:T(128)S(6)} %select_n.118), kind=kOutput, calls=%fused_computation.3.clone.1 | convolution fusion | flops 243124224 | bytes 1069060 | tf_op jit(solution)/shard_map/while/body/eval_jaxpr/tjd,kd->tjk/dot_general | solution.py:87
  217.3 4.1 %fusion.66 = f32[56,256]{1,0:T(8,128)S(1)} fusion(bf16[56,64,128]{2,1,0:T(8,128)(2,1)} %get-tuple-element.649, f32[56,64]{1,0:T(8,128)S(1)} %get-tuple-element.647, bf16[2048,128]{1,0:T(8,128)(2,1)S(1)} %get-tuple-element.648, s32[]{:T(128)S(6)} %select_n.118), kind=kOutput, calls=%fused_computation.3.clone.1 | convolution fusion | flops 243124224 | bytes 1069060 | tf_op jit(solution)/shard_map/while/body/eval_jaxpr/tjd,kd->tjk/dot_general | solution.py:87
  223.1 2.0 subtract_multiply_fusion
  225.2 74.7 %while.47 = (s32[]{:T(128)}, f32[56,64]{1,0:T(8,128)S(1)}, f32[56,64,128]{2,1,0:T(8,128)S(1)}, f32[2048,128]{1,0:T(8,128)S(1)}, f32[56,2048]{1,0:T(8,128)}, /*in...) while((s32[]{:T(128)}, f32[56,64]{1,0:T(8,128)S(1)}, ...), condition=%wide.region_13.14_spmd.clone, body=%wide.region_11.13_spmd.clone.sunk | while | flops 720244224 | bytes 22540532 | solution.py:129
  226.2 5.2 %fusion.75 = (bf16[56,64,256]{2,1,0:T(8,128)(2,1)}, f32[56,64]{1,0:T(8,128)S(1)}) fusion(f32[56,64]{1,0:T(8,128)S(1)} %get-tuple-element.685, f32[56,256]{1,0:T(8,128)S(1)} %constant_dynamic-slice_fusion.5, bf16[56,64,128]{2,1,0:T(8,128)(2,1)} %get-tuple-element.684, bf16[2048,128]{1,0:T(8,128)(2,1)S(1)} %get-tuple-element.683, s32[]{:T(128)S(6)} %select_n.121), kind=kOutput, calls=%fused_computation.37.clone.1 | convolution fusion | flops 249557504 | bytes 2918404 | tf_op jit(solution)/shard_map/while/body/eval_jaxpr/tjd,kd->tjk/dot_general | solution.py:87
  231.5 2.5 select_add_fusion.5
  235.6 5.2 %fusion.75 = (bf16[56,64,256]{2,1,0:T(8,128)(2,1)}, f32[56,64]{1,0:T(8,128)S(1)}) fusion(f32[56,64]{1,0:T(8,128)S(1)} %get-tuple-element.685, f32[56,256]{1,0:T(8,128)S(1)} %constant_dynamic-slice_fusion.5, bf16[56,64,128]{2,1,0:T(8,128)(2,1)} %get-tuple-element.684, bf16[2048,128]{1,0:T(8,128)(2,1)S(1)} %get-tuple-element.683, s32[]{:T(128)S(6)} %select_n.121), kind=kOutput, calls=%fused_computation.37.clone.1 | convolution fusion | flops 249557504 | bytes 2918404 | tf_op jit(solution)/shard_map/while/body/eval_jaxpr/tjd,kd->tjk/dot_general | solution.py:87
  240.8 2.5 select_add_fusion.5
  244.9 5.2 %fusion.75 = (bf16[56,64,256]{2,1,0:T(8,128)(2,1)}, f32[56,64]{1,0:T(8,128)S(1)}) fusion(f32[56,64]{1,0:T(8,128)S(1)} %get-tuple-element.685, f32[56,256]{1,0:T(8,128)S(1)} %constant_dynamic-slice_fusion.5, bf16[56,64,128]{2,1,0:T(8,128)(2,1)} %get-tuple-element.684, bf16[2048,128]{1,0:T(8,128)(2,1)S(1)} %get-tuple-element.683, s32[]{:T(128)S(6)} %select_n.121), kind=kOutput, calls=%fused_computation.37.clone.1 | convolution fusion | flops 249557504 | bytes 2918404 | tf_op jit(solution)/shard_map/while/body/eval_jaxpr/tjd,kd->tjk/dot_general | solution.py:87
  250.1 2.5 select_add_fusion.5
  254.2 5.2 %fusion.75 = (bf16[56,64,256]{2,1,0:T(8,128)(2,1)}, f32[56,64]{1,0:T(8,128)S(1)}) fusion(f32[56,64]{1,0:T(8,128)S(1)} %get-tuple-element.685, f32[56,256]{1,0:T(8,128)S(1)} %constant_dynamic-slice_fusion.5, bf16[56,64,128]{2,1,0:T(8,128)(2,1)} %get-tuple-element.684, bf16[2048,128]{1,0:T(8,128)(2,1)S(1)} %get-tuple-element.683, s32[]{:T(128)S(6)} %select_n.121), kind=kOutput, calls=%fused_computation.37.clone.1 | convolution fusion | flops 249557504 | bytes 2918404 | tf_op jit(solution)/shard_map/while/body/eval_jaxpr/tjd,kd->tjk/dot_general | solution.py:87
  259.4 2.5 select_add_fusion.5
  263.5 5.2 %fusion.75 = (bf16[56,64,256]{2,1,0:T(8,128)(2,1)}, f32[56,64]{1,0:T(8,128)S(1)}) fusion(f32[56,64]{1,0:T(8,128)S(1)} %get-tuple-element.685, f32[56,256]{1,0:T(8,128)S(1)} %constant_dynamic-slice_fusion.5, bf16[56,64,128]{2,1,0:T(8,128)(2,1)} %get-tuple-element.684, bf16[2048,128]{1,0:T(8,128)(2,1)S(1)} %get-tuple-element.683, s32[]{:T(128)S(6)} %select_n.121), kind=kOutput, calls=%fused_computation.37.clone.1 | convolution fusion | flops 249557504 | bytes 2918404 | tf_op jit(solution)/shard_map/while/body/eval_jaxpr/tjd,kd->tjk/dot_general | solution.py:87
  268.8 2.5 select_add_fusion.5
  272.8 5.2 %fusion.75 = (bf16[56,64,256]{2,1,0:T(8,128)(2,1)}, f32[56,64]{1,0:T(8,128)S(1)}) fusion(f32[56,64]{1,0:T(8,128)S(1)} %get-tuple-element.685, f32[56,256]{1,0:T(8,128)S(1)} %constant_dynamic-slice_fusion.5, bf16[56,64,128]{2,1,0:T(8,128)(2,1)} %get-tuple-element.684, bf16[2048,128]{1,0:T(8,128)(2,1)S(1)} %get-tuple-element.683, s32[]{:T(128)S(6)} %select_n.121), kind=kOutput, calls=%fused_computation.37.clone.1 | convolution fusion | flops 249557504 | bytes 2918404 | tf_op jit(solution)/shard_map/while/body/eval_jaxpr/tjd,kd->tjk/dot_general | solution.py:87
  278.1 2.5 select_add_fusion.5
  282.1 5.2 %fusion.75 = (bf16[56,64,256]{2,1,0:T(8,128)(2,1)}, f32[56,64]{1,0:T(8,128)S(1)}) fusion(f32[56,64]{1,0:T(8,128)S(1)} %get-tuple-element.685, f32[56,256]{1,0:T(8,128)S(1)} %constant_dynamic-slice_fusion.5, bf16[56,64,128]{2,1,0:T(8,128)(2,1)} %get-tuple-element.684, bf16[2048,128]{1,0:T(8,128)(2,1)S(1)} %get-tuple-element.683, s32[]{:T(128)S(6)} %select_n.121), kind=kOutput, calls=%fused_computation.37.clone.1 | convolution fusion | flops 249557504 | bytes 2918404 | tf_op jit(solution)/shard_map/while/body/eval_jaxpr/tjd,kd->tjk/dot_general | solution.py:87
  287.4 2.5 select_add_fusion.5
  291.4 5.2 %fusion.75 = (bf16[56,64,256]{2,1,0:T(8,128)(2,1)}, f32[56,64]{1,0:T(8,128)S(1)}) fusion(f32[56,64]{1,0:T(8,128)S(1)} %get-tuple-element.685, f32[56,256]{1,0:T(8,128)S(1)} %constant_dynamic-slice_fusion.5, bf16[56,64,128]{2,1,0:T(8,128)(2,1)} %get-tuple-element.684, bf16[2048,128]{1,0:T(8,128)(2,1)S(1)} %get-tuple-element.683, s32[]{:T(128)S(6)} %select_n.121), kind=kOutput, calls=%fused_computation.37.clone.1 | convolution fusion | flops 249557504 | bytes 2918404 | tf_op jit(solution)/shard_map/while/body/eval_jaxpr/tjd,kd->tjk/dot_general | solution.py:87
  296.7 2.5 select_add_fusion.5
  299.9 19.1 %all_to_all.10 = f32[16,128,128]{2,1,0:T(8,128)} all-to-all(f32[16,128,128]{2,1,0:T(8,128)S(1)} %bitcast.111), channel_id=1, replica_groups=mesh['ctx'=16,'tp'=8] {'ctx'}, dimensions={0} | all-to-all | bytes 2097152 | tf_op jit(solution)/shard_map/all_to_all | solution.py:26
  320.3 14.3 %all_to_all.11 = f32[8,16,128]{2,1,0:T(8,128)S(1)} all-to-all(f32[8,16,128]{2,1,0:T(8,128)S(1)} %bitcast.113), channel_id=1, replica_groups=mesh['ctx'=16,'tp'=8] {'tp'}, dimensions={0} | all-to-all | bytes 131072 | tf_op jit(solution)/shard_map/all_to_all | solution.py:26
  (139 shorter events, 40.2 us)
Async XLA Ops:
  7.2 98.9 %all-gather.2.cloned.1.call-start = ((), (), s32[]{:S(2)}) async-start(), calls=%async_computation.3 | async-start | bytes 13926400 | tf_op jit(solution)/shard_map/all_gather | solution.py:11
  9.3 4.7 %copy-start.4 = (s32[16]{0:T(128)S(1)}, s32[16]{0:T(128)}, u32[]{:S(2)}) copy-start(s32[16]{0:T(128)} %param.23) | copy-start | bytes 196
  9.3 212.6 %reduce-scatter.2.cloned.1.call-start = ((), (), s32[]{:S(2)}) async-start(), calls=%async_computation.4 | async-start | bytes 4128768 | tf_op jit(solution)/shard_map/reduce_scatter | solution.py:76
  116.8 2.2 copy-start.6
  187.4 1.1 slice-start
  187.4 1.1 copy-start.7
  188.5 34.6 %copy-start.3 = (f32[56]{0:T(128)S(1)}, f32[56]{0:T(128)}, u32[]{:S(2)}) copy-start(f32[56]{0:T(128)} %param.21) | copy-start | bytes 676
  231.5 2.5 copy-start.1
  231.5 2.5 copy-start.5
  240.8 2.5 copy-start.1
  240.8 2.5 copy-start.5
  250.1 2.5 copy-start.1
  250.1 2.5 copy-start.5
  259.4 2.5 copy-start.1
  259.4 2.5 copy-start.5
  268.7 2.5 copy-start.1
  268.7 2.5 copy-start.5
  278.0 2.5 copy-start.1
  278.0 2.5 copy-start.5
  287.4 2.5 copy-start.1
  287.4 2.5 copy-start.5
  296.7 2.5 copy-start.1
  296.7 2.5 copy-start.5
  299.9 35.3 %copy-start = (f32[56,64,128]{2,1,0:T(8,128)}, f32[56,64,128]{2,1,0:T(8,128)S(1)}, u32[]{:S(2)}) copy-start(f32[56,64,128]{2,1,0:T(8,128)S(1)} %get-tuple-element.359) | copy-start | bytes 5505028
  299.9 35.3 %copy-start.2 = (f32[56,64]{1,0:T(8,128)}, f32[56,64]{1,0:T(8,128)S(1)}, u32[]{:S(2)}) copy-start(f32[56,64]{1,0:T(8,128)S(1)} %get-tuple-element.360) | copy-start | bytes 43012
Sparse Core Ops, SparseCore 0:
  10.7 95.3 all-gather.1
  187.6 33.9 reduce-scatter.1
where the time goes:
time: 344 us; the launch traced here: 342 us
  matrix products  137 us (40%)
  waiting for transfers between devices  92 us (27%)
  local copies, waits for them, and re-layouts  49.8 us (14%)
  blocking collectives  33.4 us (10%)
  between operations  14.9 us (4%)
  other arithmetic  14.1 us (4%)
    all_gather x1, waiting for transfers between devices, in_one_piece(): out, at, done = (lax.all_gather(both, axis, axis=dim, tiled=True), 0, [])  92 us
    dot_general x16, matrix products, raw_scores(): jnp.einsum('tjd,kd->tjk', index_q, key_block, preferred_element_type=jnp....  74.3 us
    dot_general x8, matrix products, add_block(): jnp.einsum('qhd,khd->qhk', queries_wide, key_block, preferred_element_typ...  36.8 us
    all_to_all x2, blocking collectives, summed_on_arrival(): lax.all_to_all(cut_along(array, dim, length), axis, 0, 0, tiled=True)  33.4 us
    dot_general x8, matrix products, second_pass(): jnp.einsum('tjk,kd->tjd', score_grad, key_block, preferred_element_type=j...  20 us
    dynamic_slice x16, local copies, waits for them, and re-layouts, add_block(): lax.dynamic_slice_in_dim(keys, first_key, block_keys, 0)  17.7 us
    slice x3, local copies, waits for them, and re-layouts, in_one_piece(): done.append(lax.slice_in_dim(out, at, at + a.shape[along], axis=along))  10.9 us
  transfers between devices with their start and end apart: 2, of which 1 were waited for; matrix products, arithmetic and copies ran while one was open for 11% of the time, Pallas kernels for 0%

commit v1 on v0

v1 whole, which is shorter than its diff:
```python
import math

import jax
import jax.numpy as jnp
from jax import lax
from jax.experimental import pallas as pl
from jax.experimental.pallas import tpu as pltpu
from jax.sharding import PartitionSpec as P

MESH = pl.DeviceIdType.MESH
SIDE = 4
N_CTX = SIDE * SIDE
N_TP = 8
ROWS = 448
KEYS = 128
DQK = 192
HEADS = 16
OWN = 56
HI = 64
DI = 128
FLAT = OWN * HI
WIDE = 256
LOG2E = math.log2(math.e)
LN2 = math.log(2.0)
VMEM_LIMIT = 67043328
CONTRACT_LAST = (((1,), (1,)), ((), ()))


def rem(a, b):
    return lax.rem(a, jnp.int32(b))


def div(a, b):
    return lax.div(a, jnp.int32(b))


def ring_places(ctx):
    x, y = div(ctx, SIDE), rem(ctx, SIDE)
    turn = rem(x + y, SIDE)
    return SIDE * x + turn, SIDE * y + turn


def ring_member(ring, place):
    place = rem(place + 2 * N_CTX, N_CTX)
    major = div(place, SIDE)
    minor = rem(rem(place, SIDE) - major + SIDE, SIDE)
    return SIDE * major + minor if ring < 2 else SIDE * minor + major


def kernel(
    q_hbm, k_hbm, norm_hbm, iq_hbm, iw_ref, ik_hbm, rw_ref, off_ref, map_ref,
    gq_hbm, gw_ref, gk_ref,
    qpad, kbuf, ikbuf, iq, iqt, norm, nb, wb, nsp, lg, mass, mrecv, gkt, gkst, grk, fst, frecv,
    lsem, qsem, ksend, isend, krecv, irecv, msend, mrsem, gsend, gsem, fsend, fsem, osem,
):
    ctx, tp = lax.axis_index("ctx"), lax.axis_index("tp")
    place1, place2 = ring_places(ctx)
    places = (place1, place1, place2, place2)
    turns = (1, -1, 1, -1)
    nexts = [ring_member(i, places[i] + turns[i]) for i in range(4)]

    def source(ring, slot):
        return ring_member(ring, places[ring] - turns[ring] * slot)

    local = [
        pltpu.make_async_copy(k_hbm, kbuf.at[0], lsem.at[0]),
        pltpu.make_async_copy(ik_hbm, ikbuf.at[0], lsem.at[1]),
        pltpu.make_async_copy(norm_hbm, norm, lsem.at[2]),
        pltpu.make_async_copy(iq_hbm, iq, lsem.at[3]),
    ]
    for copy in local:
        copy.start()
    q_copies = []
    for head in range(HEADS):
        first = (head // 2) * 2 * DQK + (head % 2) * 128
        q_copies.append(
            pltpu.make_async_copy(q_hbm.at[:, pl.ds(first, WIDE)], qpad.at[head], qsem.at[head])
        )
        q_copies[-1].start()

    barrier = pltpu.get_barrier_semaphore()

    def greet_ctx(d, carry):
        pl.semaphore_signal(
            barrier, inc=1, device_id={"ctx": rem(ctx + d, N_CTX)}, device_id_type=MESH
        )
        return carry

    def greet_tp(d, carry):
        pl.semaphore_signal(
            barrier, inc=1, device_id={"tp": rem(tp + d, N_TP)}, device_id_type=MESH
        )
        return carry

    lax.fori_loop(1, N_CTX, greet_ctx, 0)
    lax.fori_loop(1, N_TP, greet_tp, 0)
    pl.semaphore_wait(barrier, N_CTX + N_TP - 2)

    def send_keys(slot, half):
        for i in range(4):
            pltpu.make_async_remote_copy(
                src_ref=kbuf.at[slot, half, i],
                dst_ref=kbuf.at[slot + 1, half, i],
                send_sem=ksend,
                recv_sem=krecv.at[slot + 1, half],
                device_id={"ctx": nexts[i]},
                device_id_type=MESH,
            ).start()

    def send_index_keys(slot):
        for i in range(4):
            pltpu.make_async_remote_copy(
                src_ref=ikbuf.at[slot, :, i],
                dst_ref=ikbuf.at[slot + 1, :, i],
                send_sem=isend,
                recv_sem=irecv.at[slot + 1],
                device_id={"ctx": nexts[i]},
                device_id_type=MESH,
            ).start()

    def wait_keys(slot, half):
        pltpu.make_async_copy(kbuf.at[slot, half], kbuf.at[slot, half], krecv.at[slot, half]).wait()

    def wait_index_keys(slot):
        pltpu.make_async_copy(ikbuf.at[slot], ikbuf.at[slot], irecv.at[slot]).wait()

    local[1].wait()
    send_index_keys(0)
    local[0].wait()
    send_keys(0, 0)
    send_keys(0, 1)

    for copy in local[2:]:
        copy.wait()
    for copy in q_copies:
        copy.wait()
    lane = lax.broadcasted_iota(jnp.int32, (ROWS, 128), 1)
    for head in range(HEADS):
        cols = slice(128, 256) if head % 2 == 0 else slice(0, 128)
        kept = lane < DQK - 128 if head % 2 == 0 else lane >= 256 - DQK
        part = jnp.where(kept, qpad[head, :, cols].astype(jnp.float32), 0.0)
        qpad[head, :, cols] = part.astype(jnp.bfloat16)
        nb[head * ROWS : (head + 1) * ROWS, :] = jnp.broadcast_to(
            norm[:, head : head + 1] * LOG2E, (ROWS, 128)
        )

    diagonal = lax.broadcasted_iota(jnp.int32, (HI, HI), 0) == lax.broadcasted_iota(
        jnp.int32, (HI, HI), 1
    )

    def spread_weights(t, carry):
        row = jnp.broadcast_to(iw_ref[pl.ds(t, 1), :], (HI, HI))
        column = jnp.sum(jnp.where(diagonal, row, 0.0), axis=1, keepdims=True)
        wb[pl.ds(pl.multiple_of(t * HI, HI), HI), :] = jnp.broadcast_to(column, (HI, 128))
        return carry

    lax.fori_loop(0, OWN, spread_weights, 0)

    def turn_queries(b, carry):
        first = pl.multiple_of(b * WIDE, WIDE)
        iqt[:, pl.ds(first, WIDE)] = iq[pl.ds(first, WIDE), :].astype(jnp.float32).T.astype(jnp.bfloat16)
        return carry

    lax.fori_loop(0, FLAT // WIDE, turn_queries, 0)

    score_scale = LOG2E / math.sqrt(DQK)
    inv_root = 1.0 / math.sqrt(DI)
    half_rows = ROWS // 2

    def head_mass(slot, half, parity):
        first = pl.multiple_of(half * half_rows, half_rows)
        total = None
        for head in range(HEADS):
            col = (head // 2) * 2 * DQK + (head % 2) * 128
            keys = kbuf[slot, :, :, :, col : col + WIDE].reshape(KEYS, WIDE)
            scores = lax.dot_general(
                qpad[head, pl.ds(first, half_rows), :], keys, CONTRACT_LAST,
                preferred_element_type=jnp.float32,
            )
            norms = nb[pl.ds(pl.multiple_of(head * ROWS + first, 32), half_rows), :]
            term = jnp.exp2(scores * score_scale - norms)
            total = term if total is None else total + term
        mass[parity, pl.ds(first, half_rows), :] = total

    def first_pass(slot, half):
        keys = ikbuf[slot].reshape(KEYS, DI)

        def eight_rows(b, carry):
            rows = []
            for part in range(2):
                first = pl.multiple_of(b * 8 * HI + part * 4 * HI, 4 * HI)
                inner = lax.dot_general(
                    iq[pl.ds(first, 4 * HI), :], keys, CONTRACT_LAST,
                    preferred_element_type=jnp.float32,
                )
                v = inner * (inv_root * LOG2E)
                minus = jnp.minimum(-v, 0.0) - jnp.log2(1.0 + jnp.exp2(-jnp.abs(v)))
                nsp[slot, pl.ds(first, 4 * HI), :] = minus
                weighted = wb[pl.ds(first, 4 * HI), :] * minus
                for u in range(4):
                    rows.append(
                        jnp.sum(weighted[u * HI : (u + 1) * HI, :], axis=0, keepdims=True)
                    )
            lg[slot, pl.ds(pl.multiple_of(b * 8, 8), 8), :] = jnp.concatenate(rows, axis=0)
            return carry

        lax.fori_loop(4 * half, 4 + 3 * half, eight_rows, 0)

    def wait_mass_sent(parity):
        sent = mass.at[parity, pl.ds(0, ROWS - OWN)]
        pltpu.make_async_copy(sent, sent, msend.at[parity]).wait()

    def send_mass(slot, parity):
        for d in range(1, N_TP):
            peer = rem(tp + d, N_TP)
            pltpu.make_async_remote_copy(
                src_ref=mass.at[parity, pl.ds(pl.multiple_of(peer * OWN, 8), OWN)],
                dst_ref=mrecv.at[d, slot],
                send_sem=msend.at[parity],
                recv_sem=mrsem,
                device_id={"tp": peer},
                device_id_type=MESH,
            ).start()
        mrecv[0, slot] = mass[parity, pl.ds(pl.multiple_of(tp * OWN, 8), OWN), :]

    def step(it, carry):
        slot, half = div(it, 2), rem(it, 2)

        @pl.when(it < 2 * (N_CTX - 1))
        def _():
            @pl.when(half == 0)
            def _():
                wait_index_keys(slot)
                send_index_keys(slot)

            wait_keys(slot, half)
            send_keys(slot, half)

        @pl.when(it == 2 * N_CTX)
        def _():
            wait_index_keys(N_CTX - 1)
            wait_keys(N_CTX - 1, 0)
            wait_keys(N_CTX - 1, 1)

        now = slot - 1
        parity = rem(now, 2)

        @pl.when((half == 0) & (now >= 2))
        def _():
            wait_mass_sent(parity)

        head_mass(now, half, parity)

        @pl.when(half == 1)
        def _():
            send_mass(now, parity)

        first_pass(now, half)
        return carry

    lax.fori_loop(2, 2 * N_CTX + 2, step, 0)

    lane_row = lax.broadcasted_iota(jnp.int32, (OWN, 128), 1)
    row_pos = off_ref[0] + tp * OWN + lax.broadcasted_iota(jnp.int32, (OWN, 128), 0)
    ring_lane = rem(lax.broadcasted_iota(jnp.int32, (OWN, 128), 1), 64)

    def visible_at(slot):
        blocks = [map_ref[source(i, slot)] * KEYS for i in range(4)]
        block = jnp.where(
            ring_lane < 32,
            jnp.where(ring_lane < 16, blocks[0], blocks[1]),
            jnp.where(ring_lane < 48, blocks[2], blocks[3]),
        )
        return block + lane_row <= row_pos

    def take_max(slot, top):
        masked = jnp.where(visible_at(slot), -lg[slot], -jnp.inf)
        lg[slot] = masked
        return jnp.maximum(top, masked)

    top = lax.fori_loop(0, N_CTX, take_max, jnp.full((OWN, 128), -jnp.inf, jnp.float32))
    top = jnp.max(top, axis=1, keepdims=True)

    def take_exp(slot, total):
        term = jnp.exp2(lg[slot] - top)
        lg[slot] = term
        return total + term

    exp_total = lax.fori_loop(0, N_CTX, take_exp, jnp.zeros((OWN, 128), jnp.float32))
    exp_share = 1.0 / jnp.sum(exp_total, axis=1, keepdims=True)

    arrived = mrecv.at[pl.ds(1, N_TP - 1)]
    pltpu.make_async_copy(arrived, arrived, mrsem).wait()

    def add_mass(slot, total):
        amount = mrecv[0, slot]
        for d in range(1, N_TP):
            amount = amount + mrecv[d, slot]
        amount = jnp.where(visible_at(slot), amount, 0.0)
        mrecv[0, slot] = amount
        return total + amount

    mass_total = lax.fori_loop(0, N_CTX, add_mass, jnp.zeros((OWN, 128), jnp.float32))
    mass_total = jnp.sum(mass_total, axis=1, keepdims=True)

    def take_grad(slot, carry):
        lg[slot] = lg[slot] * exp_share - mrecv[0, slot] / mass_total
        return carry

    lax.fori_loop(0, N_CTX, take_grad, 0)

    nb[...] = jnp.zeros_like(nb)

    def key_pair(pair, carry):
        slot_a, slot_b = 2 * pair, 2 * pair + 1
        keys = ikbuf[pl.ds(slot_a, 2)].reshape(2 * KEYS, DI)
        gkt[...] = jnp.zeros_like(gkt)

        def row_block(b, carry):
            first = pl.multiple_of(b * WIDE, WIDE)
            pieces = []
            for u in range(4):
                t = b * 4 + u
                at = pl.multiple_of(first + u * HI, HI)
                weight = rw_ref[t]
                grad_a = lg[slot_a, pl.ds(t, 1), :] * weight
                grad_b = lg[slot_b, pl.ds(t, 1), :] * weight
                heads = wb[pl.ds(at, HI), :] * inv_root
                soft_a = nsp[slot_a, pl.ds(at, HI), :]
                soft_b = nsp[slot_b, pl.ds(at, HI), :]
                lanes = pl.ds(pl.multiple_of(FLAT + at, HI), HI)
                nb[lanes, :] += grad_a * soft_a + grad_b * soft_b
                part_a = (grad_a * heads) * (1.0 - jnp.exp2(soft_a))
                part_b = (grad_b * heads) * (1.0 - jnp.exp2(soft_b))
                pieces.append(
                    jnp.concatenate(
                        [part_a.astype(jnp.bfloat16), part_b.astype(jnp.bfloat16)], axis=1
                    )
                )
            score_grad = jnp.concatenate(pieces, axis=0)
            nb[pl.ds(first, WIDE), :] += jnp.dot(
                score_grad, keys, preferred_element_type=jnp.float32
            )
            gkt[...] += jnp.dot(
                iqt[:, pl.ds(first, WIDE)], score_grad, preferred_element_type=jnp.float32
            )
            return carry

        lax.fori_loop(0, FLAT // WIDE, row_block, 0)
        for part, slot in ((0, slot_a), (1, slot_b)):
            turned = gkt[:, part * KEYS : (part + 1) * KEYS].T.reshape(2, 4, 16, DI)
            gkst[slot] = turned

            def send(slot=slot):
                for i in range(4):
                    pltpu.make_async_remote_copy(
                        src_ref=gkst.at[slot, :, i],
                        dst_ref=grk.at[slot, :, i],
                        send_sem=gsend,
                        recv_sem=gsem,
                        device_id={"ctx": source(i, slot)},
                        device_id_type=MESH,
                    ).start()

            if part == 0:
                pl.when(pair > 0)(send)
            else:
                send()
        return carry

    lax.fori_loop(0, N_CTX // 2, key_pair, 0)
    out_copy = pltpu.make_async_copy(nb.at[pl.ds(0, FLAT)], gq_hbm, osem)
    out_copy.start()

    def finish_weights(r, carry):
        block = nb[pl.ds(pl.multiple_of(FLAT + r * 128, 128), 128), :]
        gw_ref[pl.ds(r, 1), :] = jnp.sum(block.T, axis=0, keepdims=True) * -LN2
        return carry

    lax.fori_loop(0, FLAT // 128, finish_weights, 0)

    came = grk.at[pl.ds(1, N_CTX - 1)]
    pltpu.make_async_copy(came, came, gsem).wait()
    own_sum = gkst[0]
    for slot in range(1, N_CTX):
        own_sum = own_sum + grk[slot]
    fst[...] = own_sum.reshape(N_TP, 16, DI)
    for d in range(1, N_TP):
        peer = rem(tp + d, N_TP)
        pltpu.make_async_remote_copy(
            src_ref=fst.at[peer],
            dst_ref=frecv.at[d],
            send_sem=fsend,
            recv_sem=fsem,
            device_id={"tp": peer},
            device_id_type=MESH,
        ).start()
    landed = frecv.at[pl.ds(1, N_TP - 1)]
    pltpu.make_async_copy(landed, landed, fsem).wait()
    total = fst[tp]
    for d in range(1, N_TP):
        total = total + frecv[d]
    gk_ref[...] = total

    out_copy.wait()
    pltpu.make_async_copy(landed, landed, fsend).wait()
    sent = kbuf.at[pl.ds(0, N_CTX - 1)]
    pltpu.make_async_copy(sent, sent, ksend).wait()
    sent = ikbuf.at[pl.ds(0, N_CTX - 1)]
    pltpu.make_async_copy(sent, sent, isend).wait()
    pltpu.make_async_copy(came, came, gsend).wait()
    wait_mass_sent(0)
    wait_mass_sent(1)


def per_device(main_q, main_k, log_norms, index_q, index_w, index_k, row_weight, offsets, key_map):
    anywhere = pl.BlockSpec(memory_space=pl.ANY)
    vmem = pl.BlockSpec(memory_space=pltpu.VMEM)
    smem = pl.BlockSpec(memory_space=pltpu.SMEM)
    f32, bf16 = jnp.float32, jnp.bfloat16
    dma = pltpu.SemaphoreType.DMA
    grad_q, grad_w, grad_k = pl.pallas_call(
        kernel,
        out_shape=(
            jax.ShapeDtypeStruct((FLAT, DI), f32),
            jax.ShapeDtypeStruct((FLAT // 128, 128), f32),
            jax.ShapeDtypeStruct((16, DI), f32),
        ),
        in_specs=[anywhere, anywhere, anywhere, anywhere, vmem, anywhere, smem, smem, smem],
        out_specs=(anywhere, vmem, vmem),
        scratch_shapes=[
            pltpu.VMEM((HEADS, ROWS, WIDE), bf16),
            pltpu.VMEM((N_CTX, 2, 4, 16, HEADS * DQK), bf16),
            pltpu.VMEM((N_CTX, 2, 4, 16, DI), bf16),
            pltpu.VMEM((FLAT, DI), bf16),
            pltpu.VMEM((DI, FLAT), bf16),
            pltpu.VMEM((ROWS, HEADS), f32),
            pltpu.VMEM((HEADS * ROWS, 128), f32),
            pltpu.VMEM((FLAT, 128), f32),
            pltpu.VMEM((N_CTX, FLAT, 128), f32),
            pltpu.VMEM((N_CTX, OWN, 128), f32),
            pltpu.VMEM((2, ROWS, 128), f32),
            pltpu.VMEM((N_TP, N_CTX, OWN, 128), f32),
            pltpu.VMEM((DI, 2 * KEYS), f32),
            pltpu.VMEM((N_CTX, 2, 4, 16, DI), f32),
            pltpu.VMEM((N_CTX, 2, 4, 16, DI), f32),
            pltpu.VMEM((N_TP, 16, DI), f32),
            pltpu.VMEM((N_TP, 16, DI), f32),
            dma((4,)),
            dma((HEADS,)),
            dma,
            dma,
            dma((N_CTX, 2)),
            dma((N_CTX,)),
            dma((2,)),
            dma,
            dma,
            dma,
            dma,
            dma,
            dma,
        ],
        compiler_params=pltpu.CompilerParams(
            collective_id=0, has_side_effects=True, vmem_limit_bytes=VMEM_LIMIT
        ),
        name="indexer_grads",
    )(
        main_q,
        main_k.reshape(2, 4, 16, HEADS * DQK),
        log_norms,
        index_q.reshape(FLAT, DI),
        index_w,
        index_k.reshape(2, 4, 16, DI),
        row_weight,
        offsets,
        key_map,
    )
    return grad_q.reshape(OWN, HI, DI), grad_w.reshape(OWN, HI), grad_k


def solution(mesh):
    placed = (
        P("ctx", "tp"),
        P("ctx", "tp"),
        P("ctx", "tp"),
        P(("ctx", "tp"), None, None),
        P(("ctx", "tp"), None),
        P("ctx", None),
        P(("ctx", "tp")),
        P("ctx"),
        P(),
    )
    return jax.shard_map(
        per_device,
        mesh=mesh,
        in_specs=placed,
        out_specs=(P(("ctx", "tp"), None, None), P(("ctx", "tp"), None), P(("ctx", "tp"), None)),
        check_vma=False,
    )
```

time: 344 us -> 141 us (0.41)
  matrix products: 137 us -> 0 us
  Pallas kernels: 0 us -> 132 us
  waiting for transfers between devices: 92 us -> 0 us
  local copies, waits for them, and re-layouts: 49.8 us -> 6.53 us
  blocking collectives: 33.4 us -> 0 us
  other arithmetic: 14.1 us -> 0 us
  between operations: 14.9 us -> 1.29 us
    dot_general x40 -> x0, matrix products: 137 us -> none  [the longest x16 74.3 us: raw_scores(): jnp.einsum('tjd,kd->tjk', index_q, key_block, preferred_element_type=jnp....]
    pallas_call x0 -> x1, Pallas kernels: none -> 132 us  [per_device(): pl.pallas_call(kernel, out_shape=(jax.ShapeDtypeStruct((FLAT, DI), f32),...]
    all_gather x1 -> x0, waiting for transfers between devices: 92 us -> none  [in_one_piece(): out, at, done = (lax.all_gather(both, axis, axis=dim, tiled=True), 0, [])]
    all_to_all x2 -> x0, blocking collectives: 33.4 us -> none  [summed_on_arrival(): lax.all_to_all(cut_along(array, dim, length), axis, 0, 0, tiled=True)]
    dynamic_slice x32 -> x0, local copies, waits for them, and re-layouts: 24.9 us -> none  [the longest x16 17.7 us: add_block(): lax.dynamic_slice_in_dim(keys, first_key, block_keys, 0)]
    slice x3 -> x0, local copies, waits for them, and re-layouts: 10.9 us -> none  [in_one_piece(): done.append(lax.slice_in_dim(out, at, at + a.shape[along], axis=along))]
    dynamic_update_slice x16 -> x0, local copies, waits for them, and re-layouts: 6.85 us -> none  [the longest x8 6.76 us: add_block(): lax.dynamic_update_slice_in_dim(running, jnp.sum(prob_terms, axis=1), fir...]
    add x18 -> x0, other arithmetic: 5.25 us -> none  [the longest x8 5.18 us: per_device(): block_pos = first_pos + jnp.arange(block_rows, dtype=jnp.int32)]
  transfers between devices with their start and end apart: 2 -> 0, of which waited for: 1 -> 0; matrix products, arithmetic and copies ran while one was open for 11% -> 0% of each run, Pallas kernels for 0% -> 0%
where the time goes in v1:
time: 141 us; the launch traced here: 140 us
  Pallas kernels  132 us (94%)
  local copies, waits for them, and re-layouts  6.53 us (5%)
    pallas_call x1, Pallas kernels, per_device(): pl.pallas_call(kernel, out_shape=(jax.ShapeDtypeStruct((FLAT, DI), f32),...  132 us
    unnamed x5, local copies, waits for them, and re-layouts  5.13 us

profile of v1, /device:TPU:1, one launch (start us, length us, event | category | flops | bytes accessed | tf_op | source)
XLA Modules:
  0.0 140.2 jit_solution(6551094822271559184)
XLA Ops:
  1.3 1.6 %copy.12.norm_hbm = f32[448,16]{1,0:T(8,128)} copy(f32[448,16]{0,1:T(8,128)} %param.11) | data formatting | bytes 57344 | tf_op args[2]
  2.9 132.4 %indexer_grads.1 = (f32[3584,128]{1,0:T(8,128)}, f32[28,128]{1,0:T(8,128)}, f32[16,128]{1,0:T(8,128)}) custom-call(bf16[448,3072]{1,0:T(8,128)(2,1)} %q_hbm.1, bf16[2,4,16,3072]{3,2,1,0:T(8,128)(2,1)} %bitcast.6, f32[448,16]{1,0:T(8,128)} %copy.12.norm_hbm, bf16[3584,128]{1,0:T(8,128)(2,1)} %bitcast.5, f32[56,64]{1,0:T(8,128)} %iw_ref.1, ...), custom_call_target="tpu_custom_call" | custom-call | tf_op jit(solution)/shard_map/indexer_grads/pallas_call | solution.py:422
  135.3 1.4 reshape.25
  136.7 0.0 copy-start
  136.7 3.0 %copy.16 = f32[56,64,128]{2,1,0:T(8,128)} copy(f32[56,64,128]{2,1,0:T(8,128)} %bitcast.4) | data formatting | bytes 3670016
  139.6 0.0 copy-done
  139.6 0.6 copy.17
Async XLA Ops:
  136.7 3.0 %copy-start = (f32[16,128]{1,0:T(8,128)S(1)}, f32[16,128]{1,0:T(8,128)}, u32[]{:S(2)}) copy-start(f32[16,128]{1,0:T(8,128)} %get-tuple-element.14) | copy-start | bytes 24580

commit v2 on v1

--- a/solution.py
+++ b/solution.py
@@ -20,6 +20,8 @@
 DI = 128
 FLAT = OWN * HI
 WIDE = 256
+BLOCK = 512
+PIECES = 4
 LOG2E = math.log2(math.e)
 LN2 = math.log(2.0)
 VMEM_LIMIT = 67043328
@@ -80,21 +82,16 @@
 
     barrier = pltpu.get_barrier_semaphore()
 
-    def greet_ctx(d, carry):
-        pl.semaphore_signal(
-            barrier, inc=1, device_id={"ctx": rem(ctx + d, N_CTX)}, device_id_type=MESH
-        )
-        return carry
-
     def greet_tp(d, carry):
         pl.semaphore_signal(
             barrier, inc=1, device_id={"tp": rem(tp + d, N_TP)}, device_id_type=MESH
         )
         return carry
 
-    lax.fori_loop(1, N_CTX, greet_ctx, 0)
+    for i in range(4):
+        pl.semaphore_signal(barrier, inc=1, device_id={"ctx": nexts[i]}, device_id_type=MESH)
     lax.fori_loop(1, N_TP, greet_tp, 0)
-    pl.semaphore_wait(barrier, N_CTX + N_TP - 2)
+    pl.semaphore_wait(barrier, 4 + N_TP - 1)
 
     def send_keys(slot, half):
         for i in range(4):
@@ -135,33 +132,24 @@
     for copy in q_copies:
         copy.wait()
     lane = lax.broadcasted_iota(jnp.int32, (ROWS, 128), 1)
+    norms_down = norm[...].T * LOG2E
     for head in range(HEADS):
         cols = slice(128, 256) if head % 2 == 0 else slice(0, 128)
         kept = lane < DQK - 128 if head % 2 == 0 else lane >= 256 - DQK
         part = jnp.where(kept, qpad[head, :, cols].astype(jnp.float32), 0.0)
         qpad[head, :, cols] = part.astype(jnp.bfloat16)
         nb[head * ROWS : (head + 1) * ROWS, :] = jnp.broadcast_to(
-            norm[:, head : head + 1] * LOG2E, (ROWS, 128)
+            norms_down[:, head : head + 1], (ROWS, 128)
         )
-
-    diagonal = lax.broadcasted_iota(jnp.int32, (HI, HI), 0) == lax.broadcasted_iota(
-        jnp.int32, (HI, HI), 1
-    )
-
-    def spread_weights(t, carry):
-        row = jnp.broadcast_to(iw_ref[pl.ds(t, 1), :], (HI, HI))
-        column = jnp.sum(jnp.where(diagonal, row, 0.0), axis=1, keepdims=True)
-        wb[pl.ds(pl.multiple_of(t * HI, HI), HI), :] = jnp.broadcast_to(column, (HI, 128))
-        return carry
-
-    lax.fori_loop(0, OWN, spread_weights, 0)
+    weights_down = iw_ref[...].T
+    for t in range(OWN):
+        wb[t * HI : (t + 1) * HI, :] = jnp.broadcast_to(weights_down[:, t : t + 1], (HI, 128))
 
     def turn_queries(b, carry):
         first = pl.multiple_of(b * WIDE, WIDE)
         iqt[:, pl.ds(first, WIDE)] = iq[pl.ds(first, WIDE), :].astype(jnp.float32).T.astype(jnp.bfloat16)
         return carry
 
-    lax.fori_loop(0, FLAT // WIDE, turn_queries, 0)
 
     score_scale = LOG2E / math.sqrt(DQK)
     inv_root = 1.0 / math.sqrt(DI)
@@ -182,7 +170,7 @@
             total = term if total is None else total + term
         mass[parity, pl.ds(first, half_rows), :] = total
 
-    def first_pass(slot, half):
+    def first_pass(slot):
         keys = ikbuf[slot].reshape(KEYS, DI)
 
         def eight_rows(b, carry):
@@ -204,7 +192,7 @@
             lg[slot, pl.ds(pl.multiple_of(b * 8, 8), 8), :] = jnp.concatenate(rows, axis=0)
             return carry
 
-        lax.fori_loop(4 * half, 4 + 3 * half, eight_rows, 0)
+        lax.fori_loop(0, OWN // 8, eight_rows, 0, unroll=7)
 
     def wait_mass_sent(parity):
         sent = mass.at[parity, pl.ds(0, ROWS - OWN)]
@@ -255,10 +243,18 @@
         def _():
             send_mass(now, parity)
 
-        first_pass(now, half)
+        @pl.when(now == 0)
+        def _():
+            lax.fori_loop(7 * half, 7 + 7 * half, turn_queries, 0)
+
+        @pl.when((half == 1) & (now > 0))
+        def _():
+            first_pass(now - 1)
+
         return carry
 
     lax.fori_loop(2, 2 * N_CTX + 2, step, 0)
+    first_pass(N_CTX - 1)
 
     lane_row = lax.broadcasted_iota(jnp.int32, (OWN, 128), 1)
     row_pos = off_ref[0] + tp * OWN + lax.broadcasted_iota(jnp.int32, (OWN, 128), 0)
@@ -289,6 +285,7 @@
     exp_total = lax.fori_loop(0, N_CTX, take_exp, jnp.zeros((OWN, 128), jnp.float32))
     exp_share = 1.0 / jnp.sum(exp_total, axis=1, keepdims=True)
 
+    nb[...] = jnp.zeros_like(nb)
     arrived = mrecv.at[pl.ds(1, N_TP - 1)]
     pltpu.make_async_copy(arrived, arrived, mrsem).wait()
 
@@ -309,44 +306,42 @@
 
     lax.fori_loop(0, N_CTX, take_grad, 0)
 
-    nb[...] = jnp.zeros_like(nb)
-
     def key_pair(pair, carry):
         slot_a, slot_b = 2 * pair, 2 * pair + 1
         keys = ikbuf[pl.ds(slot_a, 2)].reshape(2 * KEYS, DI)
         gkt[...] = jnp.zeros_like(gkt)
 
         def row_block(b, carry):
-            first = pl.multiple_of(b * WIDE, WIDE)
+            first = pl.multiple_of(b * BLOCK, BLOCK)
             pieces = []
-            for u in range(4):
-                t = b * 4 + u
+            for u in range(BLOCK // HI):
+                t = b * (BLOCK // HI) + u
                 at = pl.multiple_of(first + u * HI, HI)
                 weight = rw_ref[t]
                 grad_a = lg[slot_a, pl.ds(t, 1), :] * weight
                 grad_b = lg[slot_b, pl.ds(t, 1), :] * weight
-                heads = wb[pl.ds(at, HI), :] * inv_root
+                heads = wb[pl.ds(at, HI), :]
                 soft_a = nsp[slot_a, pl.ds(at, HI), :]
                 soft_b = nsp[slot_b, pl.ds(at, HI), :]
                 lanes = pl.ds(pl.multiple_of(FLAT + at, HI), HI)
                 nb[lanes, :] += grad_a * soft_a + grad_b * soft_b
-                part_a = (grad_a * heads) * (1.0 - jnp.exp2(soft_a))
-                part_b = (grad_b * heads) * (1.0 - jnp.exp2(soft_b))
+                part_a = (grad_a * inv_root * heads) * (1.0 - jnp.exp2(soft_a))
+                part_b = (grad_b * inv_root * heads) * (1.0 - jnp.exp2(soft_b))
                 pieces.append(
                     jnp.concatenate(
                         [part_a.astype(jnp.bfloat16), part_b.astype(jnp.bfloat16)], axis=1
                     )
                 )
             score_grad = jnp.concatenate(pieces, axis=0)
-            nb[pl.ds(first, WIDE), :] += jnp.dot(
+            nb[pl.ds(first, BLOCK), :] += jnp.dot(
                 score_grad, keys, preferred_element_type=jnp.float32
             )
             gkt[...] += jnp.dot(
-                iqt[:, pl.ds(first, WIDE)], score_grad, preferred_element_type=jnp.float32
+                iqt[:, pl.ds(first, BLOCK)], score_grad, preferred_element_type=jnp.float32
             )
             return carry
 
-        lax.fori_loop(0, FLAT // WIDE, row_block, 0)
+        lax.fori_loop(0, FLAT // BLOCK, row_block, 0, unroll=FLAT // BLOCK)
         for part, slot in ((0, slot_a), (1, slot_b)):
             turned = gkt[:, part * KEYS : (part + 1) * KEYS].T.reshape(2, 4, 16, DI)
             gkst[slot] = turned
@@ -374,7 +369,9 @@
 
     def finish_weights(r, carry):
         block = nb[pl.ds(pl.multiple_of(FLAT + r * 128, 128), 128), :]
-        gw_ref[pl.ds(r, 1), :] = jnp.sum(block.T, axis=0, keepdims=True) * -LN2
+        row = jnp.sum(block.T, axis=0, keepdims=True) * -LN2
+        gw_ref[pl.ds(2 * r, 1), :] = row[:, :HI]
+        gw_ref[pl.ds(2 * r + 1, 1), :] = row[:, HI:]
         return carry
 
     lax.fori_loop(0, FLAT // 128, finish_weights, 0)
@@ -413,6 +410,22 @@
     wait_mass_sent(1)
 
 
+def hand_over(gq_in, gw_in, gk_in, gq_out, gw_out, gk_out, gq, gw, gk, in_sems, out_sems):
+    rows = FLAT // PIECES
+    pieces = [pl.ds(i * rows, rows) for i in range(PIECES)]
+    steps = [(gq_in.at[p], gq.at[p], gq_out.at[p]) for p in pieces]
+    steps += [(gw_in, gw, gw_out), (gk_in, gk, gk_out)]
+    taken = [pltpu.make_async_copy(a, b, in_sems.at[n]) for n, (a, b, c) in enumerate(steps)]
+    given = [pltpu.make_async_copy(b, c, out_sems.at[n]) for n, (a, b, c) in enumerate(steps)]
+    for copy in taken:
+        copy.start()
+    for arrival, copy in zip(taken, given):
+        arrival.wait()
+        copy.start()
+    for copy in given:
+        copy.wait()
+
+
 def per_device(main_q, main_k, log_norms, index_q, index_w, index_k, row_weight, offsets, key_map):
     anywhere = pl.BlockSpec(memory_space=pl.ANY)
     vmem = pl.BlockSpec(memory_space=pltpu.VMEM)
@@ -423,7 +436,7 @@
         kernel,
         out_shape=(
             jax.ShapeDtypeStruct((FLAT, DI), f32),
-            jax.ShapeDtypeStruct((FLAT // 128, 128), f32),
+            jax.ShapeDtypeStruct((OWN, HI), f32),
             jax.ShapeDtypeStruct((16, DI), f32),
         ),
         in_specs=[anywhere, anywhere, anywhere, anywhere, vmem, anywhere, smem, smem, smem],
@@ -434,7 +447,7 @@
             pltpu.VMEM((N_CTX, 2, 4, 16, DI), bf16),
             pltpu.VMEM((FLAT, DI), bf16),
             pltpu.VMEM((DI, FLAT), bf16),
-            pltpu.VMEM((ROWS, HEADS), f32),
+            pltpu.VMEM((HEADS, ROWS), f32),
             pltpu.VMEM((HEADS * ROWS, 128), f32),
             pltpu.VMEM((FLAT, 128), f32),
             pltpu.VMEM((N_CTX, FLAT, 128), f32),
@@ -467,7 +480,7 @@
     )(
         main_q,
         main_k.reshape(2, 4, 16, HEADS * DQK),
-        log_norms,
+        log_norms.T,
         index_q.reshape(FLAT, DI),
         index_w,
         index_k.reshape(2, 4, 16, DI),
@@ -475,7 +488,25 @@
         offsets,
         key_map,
     )
-    return grad_q.reshape(OWN, HI, DI), grad_w.reshape(OWN, HI), grad_k
+    grad_q, grad_w, grad_k = pl.pallas_call(
+        hand_over,
+        out_shape=(
+            jax.ShapeDtypeStruct((FLAT, DI), f32),
+            jax.ShapeDtypeStruct((OWN, HI), f32),
+            jax.ShapeDtypeStruct((16, DI), f32),
+        ),
+        in_specs=[anywhere] * 3,
+        out_specs=(anywhere,) * 3,
+        scratch_shapes=[
+            pltpu.VMEM((FLAT, DI), f32),
+            pltpu.VMEM((OWN, HI), f32),
+            pltpu.VMEM((16, DI), f32),
+            dma((PIECES + 2,)),
+            dma((PIECES + 2,)),
+        ],
+        name="hand_over",
+    )(grad_q, grad_w, grad_k)
+    return grad_q.reshape(OWN, HI, DI), grad_w, grad_k
 
 
 def solution(mesh):

time: 141 us -> 117 us (0.83)
  Pallas kernels: 132 us -> 115 us
  local copies, waits for them, and re-layouts: 6.53 us -> 0 us
    pallas_call x1, Pallas kernels: 132 us -> 113 us  [per_device(): pl.pallas_call(kernel, out_shape=(jax.ShapeDtypeStruct((FLAT, DI), f32),...]
    unnamed x5 -> x0, local copies, waits for them, and re-layouts: 5.13 us -> none
    pallas_call x0 -> x1, Pallas kernels: none -> 2.35 us  [per_device(): pl.pallas_call(hand_over, out_shape=(jax.ShapeDtypeStruct((FLAT, DI), f32...]
where the time goes in v2:
time: 117 us
  Pallas kernels  115 us (98%)
  between operations  1.29 us (1%)
    pallas_call x1, Pallas kernels, per_device(): pl.pallas_call(kernel, out_shape=(jax.ShapeDtypeStruct((FLAT, DI), f32),...  113 us
    pallas_call x1, Pallas kernels, per_device(): pl.pallas_call(hand_over, out_shape=(jax.ShapeDtypeStruct((FLAT, DI), f32...  2.35 us

profile of v2, /device:TPU:1, one launch (start us, length us, event | category | flops | bytes accessed | tf_op | source)
XLA Modules:
  0.0 116.7 jit_solution(6057890239985891905)
XLA Ops:
  1.3 113.0 %indexer_grads.1 = (f32[3584,128]{1,0:T(8,128)}, f32[56,64]{1,0:T(8,128)}, f32[16,128]{1,0:T(8,128)}) custom-call(bf16[448,3072]{1,0:T(8,128)(2,1)} %q_hbm.1, bf16[2,4,16,3072]{3,2,1,0:T(8,128)(2,1)} %bitcast.6, f32[16,448]{1,0:T(8,128)} %bitcast.7, bf16[3584,128]{1,0:T(8,128)(2,1)} %bitcast.5, f32[56,64]{1,0:T(8,128)} %iw_ref.1, ...), custom_call_target="tpu_custom_call" | custom-call | tf_op jit(solution)/shard_map/indexer_grads/pallas_call | solution.py:435
  114.3 2.3 %hand_over.1 = (f32[3584,128]{1,0:T(8,128)}, f32[56,64]{1,0:T(8,128)}, f32[16,128]{1,0:T(8,128)}) custom-call(f32[3584,128]{1,0:T(8,128)} %get-tuple-element.9.gq_in, f32[56,64]{1,0:T(8,128)} %get-tuple-element.10.gw_in, f32[16,128]{1,0:T(8,128)} %get-tuple-element.11.gk_in), custom_call_target="tpu_custom_call" | custom-call | tf_op jit(solution)/shard_map/hand_over/pallas_call | solution.py:491

commit v3 on v2

v3 whole, which is shorter than its diff:
```python
import math

import jax
import jax.numpy as jnp
from jax import lax
from jax.experimental import pallas as pl
from jax.experimental.pallas import tpu as pltpu
from jax.sharding import PartitionSpec as P

MESH = pl.DeviceIdType.MESH
SIDE = 4
N_CTX = SIDE * SIDE
N_TP = 8
ROWS = 448
KEYS = 128
DQK = 192
HEADS = 16
OWN = 56
HI = 64
DI = 128
FLAT = OWN * HI
WIDE = 256
BLOCK = 512
PIECES = 4
SLOTS = 8
LAST = 24
GUEST_A = 16
GUEST_B = 21
TASKS_OWN = (2, 3, 4, 5, 8, 9, 12, 13, 14, 15, 16, 17, 20, 21, 24, 24)
TASKS_GUEST_A = (16, 17, 17, 18, 18, 19, 20, 24)
TASKS_GUEST_B = (21, 21, 21, 22, 22, 22, 22, 24)
TASKS_FIRST = (4, 5, 6, 6, 7, 7, 8, 9, 10, 10, 11, 11, 12, 13, 14, 15)
LOG2E = math.log2(math.e)
LN2 = math.log(2.0)
VMEM_LIMIT = 67043328
CONTRACT_LAST = (((1,), (1,)), ((), ()))


def rem(a, b):
    return lax.rem(a, jnp.int32(b))


def div(a, b):
    return lax.div(a, jnp.int32(b))


def at_least(i, thresholds):
    count = jnp.int32(0)
    for t in thresholds:
        count = count + (i >= t).astype(jnp.int32)
    return count


def kernel(
    q_hbm, k_hbm, norm_hbm, iq_hbm, iw_ref, ik_hbm, rw_ref, off_ref, map_ref,
    gq_hbm, gw_ref, gk_ref,
    qbuf, kbuf, relay, ikn, iq, iqt, norm, nb, wb, nsp, lg, mass, mrecv, mguest, mside, gkt, grk, fst, frecv,
    lsem, yrecv, xrecv, orecv, qrecv, nrecv, irecv, mrsem, mgsem, mssem, gsem, fsem,
    ksend, rsend, qsend, nsend, isend, msend, mssend, gsend, fsend, osem,
):
    ctx, tp = lax.axis_index("ctx"), lax.axis_index("tp")
    x, y = div(ctx, SIDE), rem(ctx, SIDE)
    side = 1 - 2 * div(tp, N_TP // 2)

    def column(dx, dy):
        return SIDE * rem(x + dx + 2 * SIDE, SIDE) + rem(y + dy + 2 * SIDE, SIDE)

    up, down, right, left = column(0, 1), column(0, -1), column(1, 0), column(-1, 0)

    def source(slot, half):
        other, opposite, hops = div(slot, SLOTS), div(rem(slot, SLOTS), SIDE), rem(slot, SIDE)
        return column(2 * opposite - other * side, hops * (1 if half else -1))

    def remote(src, dst, send, recv, **where):
        return pltpu.make_async_remote_copy(
            src_ref=src, dst_ref=dst, send_sem=send, recv_sem=recv, device_id=where,
            device_id_type=MESH,
        )

    def wait_for(ref, sem):
        pltpu.make_async_copy(ref, ref, sem).wait()

    local = [
        pltpu.make_async_copy(k_hbm, kbuf.at[0], lsem.at[0]),
        pltpu.make_async_copy(ik_hbm.at[tp], ikn.at[ctx, tp], lsem.at[1]),
        pltpu.make_async_copy(norm_hbm, norm.at[2], lsem.at[2]),
        pltpu.make_async_copy(q_hbm, qbuf.at[0], lsem.at[3]),
        pltpu.make_async_copy(iq_hbm, iq, lsem.at[4]),
    ]
    for copy in local:
        copy.start()
    barrier = pltpu.get_barrier_semaphore()
    for d in range(1, SIDE):
        for peer in (column(d, 0), column(0, d)):
            pl.semaphore_signal(barrier, inc=1, device_id={"ctx": peer}, device_id_type=MESH)
    for d in range(1, N_TP):
        pl.semaphore_signal(
            barrier, inc=1, device_id={"tp": rem(tp + d, N_TP)}, device_id_type=MESH
        )
    pl.semaphore_wait(barrier, 2 * (SIDE - 1) + N_TP - 1)

    def send_y(slot, k):
        for half, peer in ((0, up), (1, down)):
            remote(
                kbuf.at[slot, half, k], kbuf.at[slot + 1, half, k], ksend, yrecv.at[slot + 1, k],
                ctx=peer,
            ).start()

    local[0].wait()
    for k in range(4):
        for half, peer in ((0, right), (1, left)):
            remote(
                kbuf.at[0, half, k], relay.at[half, k], rsend, xrecv.at[k], ctx=peer
            ).start()
        send_y(0, k)
    local[1].wait()
    for d in range(1, SIDE):
        remote(
            ikn.at[ctx, tp], ikn.at[ctx, tp], isend.at[0], irecv.at[0], ctx=column(0, d)
        ).start()
    local[2].wait()
    remote(norm.at[2], norm.at[0], nsend, nrecv, ctx=left).start()
    remote(norm.at[2], norm.at[1], nsend, nrecv, ctx=right).start()

    def spread_norms(kind, values):
        turned = values.T * LOG2E
        for head in range(HEADS):
            nb[kind, head * ROWS : (head + 1) * ROWS, :] = jnp.broadcast_to(
                turned[:, head : head + 1], (ROWS, 128)
            )

    spread_norms(0, norm[2])
    own_x = pl.ds(SIDE * x, SIDE)
    wait_for(ikn.at[pl.ds(0, SIDE - 1), 0], irecv.at[0])
    for d in range(1, SIDE):
        remote(
            ikn.at[own_x, tp], ikn.at[own_x, tp], isend.at[1], irecv.at[1], ctx=column(d, 0)
        ).start()
    weights_down = iw_ref[...].T
    for t in range(OWN):
        wb[t * HI : (t + 1) * HI, :] = jnp.broadcast_to(weights_down[:, t : t + 1], (HI, 128))
    wait_for(ikn.at[pl.ds(0, N_CTX - SIDE), 0], irecv.at[1])
    for d in range(1, N_TP):
        remote(
            ikn.at[:, tp], ikn.at[:, tp], isend.at[2], irecv.at[2], tp=rem(tp + d, N_TP)
        ).start()
    local[3].wait()
    local[4].wait()

    def turn_queries(b, carry):
        first = pl.multiple_of(b * WIDE, WIDE)
        iqt[:, pl.ds(first, WIDE)] = iq[pl.ds(first, WIDE), :].astype(jnp.float32).T.astype(jnp.bfloat16)
        return carry

    score_scale = LOG2E / math.sqrt(DQK)
    inv_root = 1.0 / math.sqrt(DI)
    quarter = ROWS // 4
    low = lax.broadcasted_iota(jnp.int32, (KEYS, 128), 1) < 64
    low = jnp.where(low, 1.0, 0.0).astype(jnp.bfloat16)
    high = (1.0 - low.astype(jnp.float32)).astype(jnp.bfloat16)

    def head_mass(kind, slot, part):
        firsts = [
            pl.multiple_of(part * quarter, 16),
            pl.multiple_of(part * quarter + ROWS // 2, 16),
        ]
        total = None
        for pair in range(HEADS // 2):
            base = pair * 2 * DQK
            tiles = [
                kbuf[slot, :, :, :, base + 128 * j : base + 128 * (j + 1)].reshape(KEYS, 128)
                for j in range(3)
            ]
            keys = [
                jnp.concatenate([tiles[0], tiles[1] * low], axis=1),
                jnp.concatenate([tiles[1] * high, tiles[2]], axis=1),
            ]
            for u in range(2):
                col = base + 128 * u
                queries = jnp.concatenate(
                    [qbuf[kind, pl.ds(f, quarter), col : col + WIDE] for f in firsts], axis=0
                )
                at = (2 * pair + u) * ROWS
                norms = jnp.concatenate(
                    [nb[kind, pl.ds(pl.multiple_of(at + f, 16), quarter), :] for f in firsts], axis=0
                )
                scores = lax.dot_general(
                    queries, keys[u], CONTRACT_LAST, preferred_element_type=jnp.float32
                )
                term = jnp.exp2(scores * score_scale - norms)
                total = term if total is None else total + term
        number = (kind * SLOTS + slot) * 2 + part
        mass[number] = total.reshape(4, OWN, 128)
        for j in range(4):
            peer = 2 * part + j % 2 + 4 * (j // 2)
            away = rem(tp - peer + N_TP, N_TP)
            if kind:
                landing, recv = mguest.at[away, slot], mgsem.at[div(slot, SLOTS - 1)]
            else:
                landing, recv = mrecv.at[away, slot], mrsem

            @pl.when(peer != tp)
            def _():
                remote(mass.at[number, j], landing, msend, recv, tp=peer).start()

            @pl.when(peer == tp)
            def _():
                landing[...] = mass[number, j]

    def first_pass(slot):
        keys = jnp.concatenate(
            [
                ikn[source(slot, 0), 0:4].reshape(KEYS // 2, DI),
                ikn[source(slot, 1), 4:8].reshape(KEYS // 2, DI),
            ],
            axis=0,
        )

        def eight_rows(b, carry):
            rows = []
            for part in range(2):
                first = pl.multiple_of(b * 8 * HI + part * 4 * HI, 4 * HI)
                inner = lax.dot_general(
                    iq[pl.ds(first, 4 * HI), :], keys, CONTRACT_LAST,
                    preferred_element_type=jnp.float32,
                )
                v = inner * (inv_root * LOG2E)
                minus = jnp.minimum(-v, 0.0) - jnp.log2(1.0 + jnp.exp2(-jnp.abs(v)))
                nsp[slot, pl.ds(first, 4 * HI), :] = minus
                weighted = wb[pl.ds(first, 4 * HI), :] * minus
                for u in range(4):
                    rows.append(
                        jnp.sum(weighted[u * HI : (u + 1) * HI, :], axis=0, keepdims=True)
                    )
            lg[slot, pl.ds(pl.multiple_of(b * 8, 8), 8), :] = jnp.concatenate(rows, axis=0)
            return carry

        lax.fori_loop(0, OWN // 8, eight_rows, 0, unroll=7)

    def add_guests(slot):
        amount = mguest[0, slot]
        for d in range(1, N_TP):
            amount = amount + mguest[d, slot]
        mguest[0, slot] = amount

    def run_tasks(i, thresholds, task):
        def one(m, carry):
            task(m)
            return carry

        lax.fori_loop(at_least(i - 1, thresholds), at_least(i, thresholds), one, 0)

    def step(i, carry):
        k = rem(i, 4)

        @pl.when(i < LAST)
        def _():
            slot = SIDE * div(i, LAST // 2) + div(rem(i, LAST // 2), 4) + 1
            wait_for(kbuf.at[slot, :, k], yrecv.at[slot, k])

            @pl.when(rem(slot, SIDE) < SIDE - 1)
            def _():
                send_y(slot, k)

        @pl.when(i < 4)
        def _():
            wait_for(relay.at[:, k], xrecv.at[k])
            for half, peer in ((0, right), (1, left)):
                remote(
                    relay.at[half, k], kbuf.at[SIDE, half, k], rsend, orecv.at[k], ctx=peer
                ).start()

        @pl.when(i == 3)
        def _():
            for part in range(2):
                for first, peer in ((0, left), (ROWS // 2, right)):
                    rows = pl.ds(first + part * quarter, quarter)
                    remote(
                        qbuf.at[0, rows], qbuf.at[1, rows], qsend, qrecv.at[part], ctx=peer
                    ).start()

        @pl.when((i >= 8) & (i < 12))
        def _():
            wait_for(kbuf.at[SIDE, :, k], orecv.at[k])
            send_y(SIDE, k)

        @pl.when(i == 3)
        def _():
            lax.fori_loop(0, FLAT // WIDE, turn_queries, 0)

        @pl.when(i == 4)
        def _():
            wait_for(ikn.at[:, pl.ds(0, N_TP - 1)], irecv.at[2])

        @pl.when(i == GUEST_A)
        def _():
            wait_for(norm.at[pl.ds(0, 2)], nrecv)
            nearer = lax.broadcasted_iota(jnp.int32, (HEADS, ROWS), 1) < ROWS // 2
            spread_norms(1, jnp.where(nearer, norm[0], norm[1]))
            wait_for(qbuf.at[1, pl.ds(0, 2 * quarter)], qrecv.at[0])

        @pl.when(i == GUEST_B)
        def _():
            wait_for(qbuf.at[1, pl.ds(0, 2 * quarter)], qrecv.at[1])

        @pl.when(i == LAST)
        def _():
            wait_for(mguest.at[pl.ds(1, N_TP - 1), pl.ds(0, SLOTS - 1)], mgsem.at[0])
            for slot in range(SLOTS - 1):
                add_guests(slot)
            early = pl.ds(0, SLOTS - 1)
            remote(
                mguest.at[0, early], mside.at[early], mssend, mssem.at[0], ctx=column(side, 0)
            ).start()

        run_tasks(i, TASKS_GUEST_A, lambda m: head_mass(1, m, 0))
        run_tasks(i, TASKS_GUEST_B, lambda m: head_mass(1, m, 1))
        run_tasks(i, TASKS_OWN, lambda m: head_mass(0, div(m, 2), rem(m, 2)))
        run_tasks(i, TASKS_FIRST, first_pass)
        return carry

    lax.fori_loop(0, LAST + 1, step, 0)
    nb[0] = jnp.zeros_like(nb[0])
    wait_for(mguest.at[pl.ds(1, N_TP - 1), SLOTS - 1], mgsem.at[1])
    add_guests(SLOTS - 1)
    remote(
        mguest.at[0, SLOTS - 1], mside.at[SLOTS - 1], mssend, mssem.at[1], ctx=column(side, 0)
    ).start()

    lane = lax.broadcasted_iota(jnp.int32, (OWN, 128), 1)
    row_pos = off_ref[0] + tp * OWN + lax.broadcasted_iota(jnp.int32, (OWN, 128), 0)

    def visible_at(slot):
        block = jnp.where(
            lane < 64, map_ref[source(slot, 0)] * KEYS, map_ref[source(slot, 1)] * KEYS
        )
        return block + lane <= row_pos

    def take_max(slot, top):
        masked = jnp.where(visible_at(slot), -lg[slot], -jnp.inf)
        lg[slot] = masked
        return jnp.maximum(top, masked)

    top = lax.fori_loop(0, N_CTX, take_max, jnp.full((OWN, 128), -jnp.inf, jnp.float32))
    top = jnp.max(top, axis=1, keepdims=True)

    def take_exp(slot, total):
        term = jnp.exp2(lg[slot] - top)
        lg[slot] = term
        return total + term

    exp_total = lax.fori_loop(0, N_CTX, take_exp, jnp.zeros((OWN, 128), jnp.float32))
    exp_share = 1.0 / jnp.sum(exp_total, axis=1, keepdims=True)

    wait_for(mrecv.at[pl.ds(1, N_TP - 1)], mrsem)

    def add_own(slot, total):
        amount = mrecv[0, slot]
        for d in range(1, N_TP):
            amount = amount + mrecv[d, slot]
        amount = jnp.where(visible_at(slot), amount, 0.0)
        mrecv[0, slot] = amount
        return total + amount

    def add_side(slot, total):
        amount = jnp.where(visible_at(SLOTS + slot), mside[slot], 0.0)
        mrecv[1, slot] = amount
        return total + amount

    mass_total = lax.fori_loop(0, SLOTS, add_own, jnp.zeros((OWN, 128), jnp.float32))
    wait_for(mside.at[pl.ds(0, SLOTS - 1)], mssem.at[0])
    wait_for(mside.at[SLOTS - 1], mssem.at[1])
    mass_total = lax.fori_loop(0, SLOTS, add_side, mass_total)
    mass_total = jnp.sum(mass_total, axis=1, keepdims=True)

    def take_grad(slot, carry):
        amount = mrecv[div(slot, SLOTS), rem(slot, SLOTS)]
        lg[slot] = lg[slot] * exp_share - amount / mass_total
        return carry

    lax.fori_loop(0, N_CTX, take_grad, 0)

    def key_pair(pair, carry):
        slot_a, slot_b = 2 * pair, 2 * pair + 1
        keys = jnp.concatenate(
            [
                ikn[source(slot, half), 4 * half : 4 * half + 4].reshape(KEYS // 2, DI)
                for slot in (slot_a, slot_b)
                for half in range(2)
            ],
            axis=0,
        )
        gkt[...] = jnp.zeros_like(gkt)

        def row_block(b, carry):
            first = pl.multiple_of(b * BLOCK, BLOCK)
            pieces = []
            for u in range(BLOCK // HI):
                t = b * (BLOCK // HI) + u
                at = pl.multiple_of(first + u * HI, HI)
                weight = rw_ref[t]
                grad_a = lg[slot_a, pl.ds(t, 1), :] * weight
                grad_b = lg[slot_b, pl.ds(t, 1), :] * weight
                heads = wb[pl.ds(at, HI), :]
                soft_a = nsp[slot_a, pl.ds(at, HI), :]
                soft_b = nsp[slot_b, pl.ds(at, HI), :]
                lanes = pl.ds(pl.multiple_of(FLAT + at, HI), HI)
                nb[0, lanes, :] += grad_a * soft_a + grad_b * soft_b
                part_a = (grad_a * inv_root * heads) * (1.0 - jnp.exp2(soft_a))
                part_b = (grad_b * inv_root * heads) * (1.0 - jnp.exp2(soft_b))
                pieces.append(
                    jnp.concatenate(
                        [part_a.astype(jnp.bfloat16), part_b.astype(jnp.bfloat16)], axis=1
                    )
                )
            score_grad = jnp.concatenate(pieces, axis=0)
            nb[0, pl.ds(first, BLOCK), :] += jnp.dot(
                score_grad, keys, preferred_element_type=jnp.float32
            )
            gkt[...] += jnp.dot(
                iqt[:, pl.ds(first, BLOCK)], score_grad, preferred_element_type=jnp.float32
            )
            return carry

        lax.fori_loop(0, FLAT // BLOCK, row_block, 0, unroll=FLAT // BLOCK)
        at = pl.multiple_of(pair * 2 * KEYS, 2 * KEYS)
        nb[1, pl.ds(at, 2 * KEYS), :] = gkt[...].T
        for part, slot in ((0, slot_a), (1, slot_b)):

            def send(part=part, slot=slot):
                for half in range(2):
                    rows = pl.ds(pl.multiple_of(at + part * KEYS + half * 64, 64), 64)
                    remote(
                        nb.at[1, rows], grk.at[rows], gsend, gsem, ctx=source(slot, half)
                    ).start()

            if part == 0:
                pl.when(pair > 0)(send)
            else:
                send()
        return carry

    lax.fori_loop(0, N_CTX // 2, key_pair, 0)
    out_copy = pltpu.make_async_copy(nb.at[0, pl.ds(0, FLAT)], gq_hbm, osem)
    out_copy.start()

    def finish_weights(r, carry):
        block = nb[0, pl.ds(pl.multiple_of(FLAT + r * 128, 128), 128), :]
        row = jnp.sum(block.T, axis=0, keepdims=True) * -LN2
        gw_ref[pl.ds(2 * r, 1), :] = row[:, :HI]
        gw_ref[pl.ds(2 * r + 1, 1), :] = row[:, HI:]
        return carry

    lax.fori_loop(0, FLAT // 128, finish_weights, 0)

    came = grk.at[pl.ds(KEYS, (N_CTX - 1) * KEYS)]
    wait_for(came, gsem)
    own_sum = nb[1, 0:KEYS, :]
    for slot in range(1, N_CTX):
        own_sum = own_sum + grk[slot * KEYS : (slot + 1) * KEYS, :]
    fst[...] = own_sum.reshape(N_TP, 16, DI)
    for d in range(1, N_TP):
        peer = rem(tp + d, N_TP)
        remote(fst.at[peer], frecv.at[d], fsend, fsem, tp=peer).start()
    landed = frecv.at[pl.ds(1, N_TP - 1)]
    wait_for(landed, fsem)
    total = fst[tp]
    for d in range(1, N_TP):
        total = total + frecv[d]
    gk_ref[...] = total

    out_copy.wait()
    wait_for(landed, fsend)
    wait_for(came, gsend)
    wait_for(kbuf.at[pl.ds(0, SLOTS - 2)], ksend)
    wait_for(kbuf.at[pl.ds(0, 2)], rsend)
    wait_for(qbuf.at[1], qsend)
    wait_for(norm.at[pl.ds(0, 2)], nsend)
    wait_for(ikn.at[pl.ds(0, SIDE - 1), 0], isend.at[0])
    wait_for(ikn.at[pl.ds(0, N_CTX - SIDE), 0], isend.at[1])
    wait_for(ikn.at[:, pl.ds(0, N_TP - 1)], isend.at[2])
    wait_for(mside, mssend)
    wait_for(mass.at[pl.ds(0, 4 * (N_TP - 1))], msend)


def hand_over(gq_in, gw_in, gk_in, gq_out, gw_out, gk_out, gq, gw, gk, in_sems, out_sems):
    rows = FLAT // PIECES
    pieces = [pl.ds(i * rows, rows) for i in range(PIECES)]
    steps = [(gq_in.at[p], gq.at[p], gq_out.at[p]) for p in pieces]
    steps += [(gw_in, gw, gw_out), (gk_in, gk, gk_out)]
    taken = [pltpu.make_async_copy(a, b, in_sems.at[n]) for n, (a, b, c) in enumerate(steps)]
    given = [pltpu.make_async_copy(b, c, out_sems.at[n]) for n, (a, b, c) in enumerate(steps)]
    for copy in taken:
        copy.start()
    for arrival, copy in zip(taken, given):
        arrival.wait()
        copy.start()
    for copy in given:
        copy.wait()


def per_device(main_q, main_k, log_norms, index_q, index_w, index_k, row_weight, offsets, key_map):
    anywhere = pl.BlockSpec(memory_space=pl.ANY)
    vmem = pl.BlockSpec(memory_space=pltpu.VMEM)
    smem = pl.BlockSpec(memory_space=pltpu.SMEM)
    f32, bf16 = jnp.float32, jnp.bfloat16
    dma = pltpu.SemaphoreType.DMA
    grad_q, grad_w, grad_k = pl.pallas_call(
        kernel,
        out_shape=(
            jax.ShapeDtypeStruct((FLAT, DI), f32),
            jax.ShapeDtypeStruct((OWN, HI), f32),
            jax.ShapeDtypeStruct((16, DI), f32),
        ),
        in_specs=[anywhere, anywhere, anywhere, anywhere, vmem, anywhere, smem, smem, smem],
        out_specs=(anywhere, vmem, vmem),
        scratch_shapes=[
            pltpu.VMEM((2, ROWS, HEADS * DQK), bf16),
            pltpu.VMEM((SLOTS, 2, 4, 16, HEADS * DQK), bf16),
            pltpu.VMEM((2, 4, 16, HEADS * DQK), bf16),
            pltpu.VMEM((N_CTX, N_TP, 16, DI), bf16),
            pltpu.VMEM((FLAT, DI), bf16),
            pltpu.VMEM((DI, FLAT), bf16),
            pltpu.VMEM((3, HEADS, ROWS), f32),
            pltpu.VMEM((2, HEADS * ROWS, 128), f32),
            pltpu.VMEM((FLAT, 128), f32),
            pltpu.VMEM((N_CTX, FLAT, 128), f32),
            pltpu.VMEM((N_CTX, OWN, 128), f32),
            pltpu.VMEM((4 * SLOTS, 4, OWN, 128), f32),
            pltpu.VMEM((N_TP, SLOTS, OWN, 128), f32),
            pltpu.VMEM((N_TP, SLOTS, OWN, 128), f32),
            pltpu.VMEM((SLOTS, OWN, 128), f32),
            pltpu.VMEM((DI, 2 * KEYS), f32),
            pltpu.VMEM((N_CTX * KEYS, DI), f32),
            pltpu.VMEM((N_TP, 16, DI), f32),
            pltpu.VMEM((N_TP, 16, DI), f32),
            dma((5,)),
            dma((SLOTS, 4)),
            dma((4,)),
            dma((4,)),
            dma((2,)),
            dma,
            dma((3,)),
            dma,
            dma((2,)),
            dma((2,)),
            dma,
            dma,
            dma,
            dma,
            dma,
            dma,
            dma((3,)),
            dma,
            dma,
            dma,
            dma,
            dma,
        ],
        compiler_params=pltpu.CompilerParams(
            collective_id=0, has_side_effects=True, vmem_limit_bytes=VMEM_LIMIT
        ),
        name="indexer_grads",
    )(
        main_q,
        main_k.reshape(2, 4, 16, HEADS * DQK),
        log_norms.T,
        index_q.reshape(FLAT, DI),
        index_w,
        index_k.reshape(N_TP, 16, DI),
        row_weight,
        offsets,
        key_map,
    )
    grad_q, grad_w, grad_k = pl.pallas_call(
        hand_over,
        out_shape=(
            jax.ShapeDtypeStruct((FLAT, DI), f32),
            jax.ShapeDtypeStruct((OWN, HI), f32),
            jax.ShapeDtypeStruct((16, DI), f32),
        ),
        in_specs=[anywhere] * 3,
        out_specs=(anywhere,) * 3,
        scratch_shapes=[
            pltpu.VMEM((FLAT, DI), f32),
            pltpu.VMEM((OWN, HI), f32),
            pltpu.VMEM((16, DI), f32),
            dma((PIECES + 2,)),
            dma((PIECES + 2,)),
        ],
        name="hand_over",
    )(grad_q, grad_w, grad_k)
    return grad_q.reshape(OWN, HI, DI), grad_w, grad_k


def solution(mesh):
    placed = (
        P("ctx", "tp"),
        P("ctx", "tp"),
        P("ctx", "tp"),
        P(("ctx", "tp"), None, None),
        P(("ctx", "tp"), None),
        P("ctx", None),
        P(("ctx", "tp")),
        P("ctx"),
        P(),
    )
    return jax.shard_map(
        per_device,
        mesh=mesh,
        in_specs=placed,
        out_specs=(P(("ctx", "tp"), None, None), P(("ctx", "tp"), None), P(("ctx", "tp"), None)),
        check_vma=False,
    )
```

time: 117 us -> 122 us (1.043)
  Pallas kernels: 115 us -> 121 us
    pallas_call x1, Pallas kernels: 113 us -> 119 us  [per_device(): pl.pallas_call(kernel, out_shape=(jax.ShapeDtypeStruct((FLAT, DI), f32),...]
where the time goes in v3:
time: 122 us
  Pallas kernels  121 us (99%)
  between operations  1.29 us (1%)
    pallas_call x1, Pallas kernels, per_device(): pl.pallas_call(kernel, out_shape=(jax.ShapeDtypeStruct((FLAT, DI), f32),...  119 us

profile of v3, /device:TPU:1, one launch (start us, length us, event | category | flops | bytes accessed | tf_op | source)
XLA Modules:
  0.0 122.2 jit_solution(7980011945211471340)
XLA Ops:
  1.3 118.6 %indexer_grads.1 = (f32[3584,128]{1,0:T(8,128)}, f32[56,64]{1,0:T(8,128)}, f32[16,128]{1,0:T(8,128)}) custom-call(bf16[448,3072]{1,0:T(8,128)(2,1)} %q_hbm.1, bf16[2,4,16,3072]{3,2,1,0:T(8,128)(2,1)} %bitcast.6, f32[16,448]{1,0:T(8,128)} %bitcast.7, bf16[3584,128]{1,0:T(8,128)(2,1)} %bitcast.5, f32[56,64]{1,0:T(8,128)} %iw_ref.1, ...), custom_call_target="tpu_custom_call" | custom-call | tf_op jit(solution)/shard_map/indexer_grads/pallas_call | solution.py:508
  119.9 2.3 %hand_over.1 = (f32[3584,128]{1,0:T(8,128)}, f32[56,64]{1,0:T(8,128)}, f32[16,128]{1,0:T(8,128)}) custom-call(f32[3584,128]{1,0:T(8,128)} %get-tuple-element.9.gq_in, f32[56,64]{1,0:T(8,128)} %get-tuple-element.10.gw_in, f32[16,128]{1,0:T(8,128)} %get-tuple-element.11.gk_in), custom_call_target="tpu_custom_call" | custom-call | tf_op jit(solution)/shard_map/hand_over/pallas_call | solution.py:575

commit v4 on v3

--- a/solution.py
+++ b/solution.py
@@ -24,11 +24,12 @@
 PIECES = 4
 SLOTS = 8
 LAST = 24
+EARLY = 4
 GUEST_A = 16
 GUEST_B = 21
 TASKS_OWN = (2, 3, 4, 5, 8, 9, 12, 13, 14, 15, 16, 17, 20, 21, 24, 24)
 TASKS_GUEST_A = (16, 17, 17, 18, 18, 19, 20, 24)
-TASKS_GUEST_B = (21, 21, 21, 22, 22, 22, 22, 24)
+TASKS_GUEST_B = (21, 21, 21, 21, 22, 22, 22, 24)
 TASKS_FIRST = (4, 5, 6, 6, 7, 7, 8, 9, 10, 10, 11, 11, 12, 13, 14, 15)
 LOG2E = math.log2(math.e)
 LN2 = math.log(2.0)
@@ -54,9 +55,9 @@
 def kernel(
     q_hbm, k_hbm, norm_hbm, iq_hbm, iw_ref, ik_hbm, rw_ref, off_ref, map_ref,
     gq_hbm, gw_ref, gk_ref,
-    qbuf, kbuf, relay, ikn, iq, iqt, norm, nb, wb, nsp, lg, mass, mrecv, mguest, mside, gkt, grk, fst, frecv,
-    lsem, yrecv, xrecv, orecv, qrecv, nrecv, irecv, mrsem, mgsem, mssem, gsem, fsem,
-    ksend, rsend, qsend, nsend, isend, msend, mssend, gsend, fsend, osem,
+    qbuf, kbuf, relay, ikn, iq, iqt, norm, nb, wb, nsp, lg, mass, mrecv, mguest, gsum, mside, mlast, share, gkt, grk, fst, frecv,
+    lsem, yrecv, xrecv, orecv, qrecv, nrecv, irecv, mrsem, mgsem, mssem, mlsem, gsem, fsem,
+    ksend, rsend, qsend, nsend, isend, msend, dsend, mssend, gsend, fsend, osem,
 ):
     ctx, tp = lax.axis_index("ctx"), lax.axis_index("tp")
     x, y = div(ctx, SIDE), rem(ctx, SIDE)
@@ -106,21 +107,26 @@
                 ctx=peer,
             ).start()
 
+    local[1].wait()
+    for d in range(1, SIDE):
+        remote(
+            ikn.at[ctx, tp], ikn.at[ctx, tp], isend.at[0], irecv.at[0], ctx=column(0, d)
+        ).start()
     local[0].wait()
+    for k in range(4):
+        send_y(0, k)
+    own_x = pl.ds(SIDE * x, SIDE)
+    wait_for(ikn.at[pl.ds(0, SIDE - 1), 0], irecv.at[0])
+    for d in range(1, SIDE):
+        remote(
+            ikn.at[own_x, tp], ikn.at[own_x, tp], isend.at[1], irecv.at[1], ctx=column(d, 0)
+        ).start()
     for k in range(4):
         for half, peer in ((0, right), (1, left)):
             remote(
                 kbuf.at[0, half, k], relay.at[half, k], rsend, xrecv.at[k], ctx=peer
             ).start()
-        send_y(0, k)
-    local[1].wait()
-    for d in range(1, SIDE):
-        remote(
-            ikn.at[ctx, tp], ikn.at[ctx, tp], isend.at[0], irecv.at[0], ctx=column(0, d)
-        ).start()
     local[2].wait()
-    remote(norm.at[2], norm.at[0], nsend, nrecv, ctx=left).start()
-    remote(norm.at[2], norm.at[1], nsend, nrecv, ctx=right).start()
 
     def spread_norms(kind, values):
         turned = values.T * LOG2E
@@ -130,12 +136,6 @@
             )
 
     spread_norms(0, norm[2])
-    own_x = pl.ds(SIDE * x, SIDE)
-    wait_for(ikn.at[pl.ds(0, SIDE - 1), 0], irecv.at[0])
-    for d in range(1, SIDE):
-        remote(
-            ikn.at[own_x, tp], ikn.at[own_x, tp], isend.at[1], irecv.at[1], ctx=column(d, 0)
-        ).start()
     weights_down = iw_ref[...].T
     for t in range(OWN):
         wb[t * HI : (t + 1) * HI, :] = jnp.broadcast_to(weights_down[:, t : t + 1], (HI, 128))
@@ -190,20 +190,30 @@
                 term = jnp.exp2(scores * score_scale - norms)
                 total = term if total is None else total + term
         number = (kind * SLOTS + slot) * 2 + part
-        mass[number] = total.reshape(4, OWN, 128)
+        mass[number] = total.reshape(4, OWN, 128).astype(jnp.bfloat16)
         for j in range(4):
             peer = 2 * part + j % 2 + 4 * (j // 2)
             away = rem(tp - peer + N_TP, N_TP)
             if kind:
-                landing, recv = mguest.at[away, slot], mgsem.at[div(slot, SLOTS - 1)]
+                landing, recv = mguest.at[away, slot], mgsem.at[div(slot, EARLY)]
+                inside = slot < SLOTS - 1
+
+                @pl.when(slot == SLOTS - 1)
+                def _():
+                    remote(
+                        mass.at[number, j], mlast.at[away], dsend, mlsem,
+                        ctx=column(1 - 2 * (j // 2), 0), tp=peer,
+                    ).start()
+
             else:
                 landing, recv = mrecv.at[away, slot], mrsem
-
-            @pl.when(peer != tp)
+                inside = slot < SLOTS
+
+            @pl.when(inside & (peer != tp))
             def _():
-                remote(mass.at[number, j], landing, msend, recv, tp=peer).start()
-
-            @pl.when(peer == tp)
+                remote(mass.at[number, j], landing, msend.at[kind], recv, tp=peer).start()
+
+            @pl.when(inside & (peer == tp))
             def _():
                 landing[...] = mass[number, j]
 
@@ -237,11 +247,18 @@
 
         lax.fori_loop(0, OWN // 8, eight_rows, 0, unroll=7)
 
-    def add_guests(slot):
-        amount = mguest[0, slot]
-        for d in range(1, N_TP):
-            amount = amount + mguest[d, slot]
-        mguest[0, slot] = amount
+    def pass_guests(batch):
+        first, count = ((0, EARLY), (EARLY, SLOTS - 1 - EARLY))[batch]
+        slots = pl.ds(first, count)
+        wait_for(mguest.at[pl.ds(1, N_TP - 1), slots], mgsem.at[batch])
+        for slot in range(first, first + count):
+            amount = mguest[0, slot].astype(jnp.float32)
+            for d in range(1, N_TP):
+                amount = amount + mguest[d, slot].astype(jnp.float32)
+            gsum[slot] = amount
+        remote(
+            gsum.at[slots], mside.at[slots], mssend, mssem.at[batch], ctx=column(side, 0)
+        ).start()
 
     def run_tasks(i, thresholds, task):
         def one(m, carry):
@@ -252,6 +269,10 @@
 
     def step(i, carry):
         k = rem(i, 4)
+
+        @pl.when(i == LAST - 1)
+        def _():
+            pass_guests(0)
 
         @pl.when(i < LAST)
         def _():
@@ -272,6 +293,8 @@
 
         @pl.when(i == 3)
         def _():
+            remote(norm.at[2], norm.at[0], nsend, nrecv, ctx=left).start()
+            remote(norm.at[2], norm.at[1], nsend, nrecv, ctx=right).start()
             for part in range(2):
                 for first, peer in ((0, left), (ROWS // 2, right)):
                     rows = pl.ds(first + part * quarter, quarter)
@@ -305,13 +328,7 @@
 
         @pl.when(i == LAST)
         def _():
-            wait_for(mguest.at[pl.ds(1, N_TP - 1), pl.ds(0, SLOTS - 1)], mgsem.at[0])
-            for slot in range(SLOTS - 1):
-                add_guests(slot)
-            early = pl.ds(0, SLOTS - 1)
-            remote(
-                mguest.at[0, early], mside.at[early], mssend, mssem.at[0], ctx=column(side, 0)
-            ).start()
+            pass_guests(1)
 
         run_tasks(i, TASKS_GUEST_A, lambda m: head_mass(1, m, 0))
         run_tasks(i, TASKS_GUEST_B, lambda m: head_mass(1, m, 1))
@@ -321,12 +338,6 @@
 
     lax.fori_loop(0, LAST + 1, step, 0)
     nb[0] = jnp.zeros_like(nb[0])
-    wait_for(mguest.at[pl.ds(1, N_TP - 1), SLOTS - 1], mgsem.at[1])
-    add_guests(SLOTS - 1)
-    remote(
-        mguest.at[0, SLOTS - 1], mside.at[SLOTS - 1], mssend, mssem.at[1], ctx=column(side, 0)
-    ).start()
-
     lane = lax.broadcasted_iota(jnp.int32, (OWN, 128), 1)
     row_pos = off_ref[0] + tp * OWN + lax.broadcasted_iota(jnp.int32, (OWN, 128), 0)
 
@@ -355,27 +366,31 @@
     wait_for(mrecv.at[pl.ds(1, N_TP - 1)], mrsem)
 
     def add_own(slot, total):
-        amount = mrecv[0, slot]
+        amount = mrecv[0, slot].astype(jnp.float32)
         for d in range(1, N_TP):
-            amount = amount + mrecv[d, slot]
+            amount = amount + mrecv[d, slot].astype(jnp.float32)
         amount = jnp.where(visible_at(slot), amount, 0.0)
-        mrecv[0, slot] = amount
+        share[slot] = amount
         return total + amount
 
     def add_side(slot, total):
         amount = jnp.where(visible_at(SLOTS + slot), mside[slot], 0.0)
-        mrecv[1, slot] = amount
+        share[SLOTS + slot] = amount
         return total + amount
 
     mass_total = lax.fori_loop(0, SLOTS, add_own, jnp.zeros((OWN, 128), jnp.float32))
-    wait_for(mside.at[pl.ds(0, SLOTS - 1)], mssem.at[0])
-    wait_for(mside.at[SLOTS - 1], mssem.at[1])
+    wait_for(mlast, mlsem)
+    amount = mlast[0].astype(jnp.float32)
+    for d in range(1, N_TP):
+        amount = amount + mlast[d].astype(jnp.float32)
+    wait_for(mside.at[pl.ds(0, EARLY)], mssem.at[0])
+    wait_for(mside.at[pl.ds(EARLY, SLOTS - 1 - EARLY)], mssem.at[1])
+    mside[SLOTS - 1] = amount
     mass_total = lax.fori_loop(0, SLOTS, add_side, mass_total)
     mass_total = jnp.sum(mass_total, axis=1, keepdims=True)
 
     def take_grad(slot, carry):
-        amount = mrecv[div(slot, SLOTS), rem(slot, SLOTS)]
-        lg[slot] = lg[slot] * exp_share - amount / mass_total
+        lg[slot] = lg[slot] * exp_share - share[slot] / mass_total
         return carry
 
     lax.fori_loop(0, N_CTX, take_grad, 0)
@@ -479,8 +494,10 @@
     wait_for(ikn.at[pl.ds(0, SIDE - 1), 0], isend.at[0])
     wait_for(ikn.at[pl.ds(0, N_CTX - SIDE), 0], isend.at[1])
     wait_for(ikn.at[:, pl.ds(0, N_TP - 1)], isend.at[2])
-    wait_for(mside, mssend)
-    wait_for(mass.at[pl.ds(0, 4 * (N_TP - 1))], msend)
+    wait_for(gsum.at[pl.ds(0, SLOTS - 1)], mssend)
+    wait_for(mlast, dsend)
+    wait_for(mrecv.at[pl.ds(0, N_TP - 1)], msend.at[0])
+    wait_for(mguest.at[pl.ds(0, N_TP - 1), pl.ds(0, SLOTS - 1)], msend.at[1])
 
 
 def hand_over(gq_in, gw_in, gk_in, gq_out, gw_out, gk_out, gq, gw, gk, in_sems, out_sems):
@@ -526,10 +543,13 @@
             pltpu.VMEM((FLAT, 128), f32),
             pltpu.VMEM((N_CTX, FLAT, 128), f32),
             pltpu.VMEM((N_CTX, OWN, 128), f32),
-            pltpu.VMEM((4 * SLOTS, 4, OWN, 128), f32),
-            pltpu.VMEM((N_TP, SLOTS, OWN, 128), f32),
-            pltpu.VMEM((N_TP, SLOTS, OWN, 128), f32),
+            pltpu.VMEM((4 * SLOTS, 4, OWN, 128), bf16),
+            pltpu.VMEM((N_TP, SLOTS, OWN, 128), bf16),
+            pltpu.VMEM((N_TP, SLOTS, OWN, 128), bf16),
             pltpu.VMEM((SLOTS, OWN, 128), f32),
+            pltpu.VMEM((SLOTS, OWN, 128), f32),
+            pltpu.VMEM((N_TP, OWN, 128), bf16),
+            pltpu.VMEM((N_CTX, OWN, 128), f32),
             pltpu.VMEM((DI, 2 * KEYS), f32),
             pltpu.VMEM((N_CTX * KEYS, DI), f32),
             pltpu.VMEM((N_TP, 16, DI), f32),
@@ -550,7 +570,9 @@
             dma,
             dma,
             dma,
+            dma,
             dma((3,)),
+            dma((2,)),
             dma,
             dma,
             dma,

time: 122 us -> 109 us (0.89)
  Pallas kernels: 121 us -> 108 us
    pallas_call x1, Pallas kernels: 119 us -> 105 us  [per_device(): pl.pallas_call(kernel, out_shape=(jax.ShapeDtypeStruct((FLAT, DI), f32),...]
where the time goes in v4:
time: 109 us
  Pallas kernels  108 us (99%)
  between operations  1.29 us (1%)
    pallas_call x1, Pallas kernels, per_device(): pl.pallas_call(kernel, out_shape=(jax.ShapeDtypeStruct((FLAT, DI), f32),...  105 us
    pallas_call x1, Pallas kernels, per_device(): pl.pallas_call(hand_over, out_shape=(jax.ShapeDtypeStruct((FLAT, DI), f32...  2.35 us

profile of v4, /device:TPU:1, one launch (start us, length us, event | category | flops | bytes accessed | tf_op | source)
XLA Modules:
  0.0 108.9 jit_solution(9408848554967633032)
XLA Ops:
  1.3 105.2 %indexer_grads.1 = (f32[3584,128]{1,0:T(8,128)}, f32[56,64]{1,0:T(8,128)}, f32[16,128]{1,0:T(8,128)}) custom-call(bf16[448,3072]{1,0:T(8,128)(2,1)} %q_hbm.1, bf16[2,4,16,3072]{3,2,1,0:T(8,128)(2,1)} %bitcast.6, f32[16,448]{1,0:T(8,128)} %bitcast.7, bf16[3584,128]{1,0:T(8,128)(2,1)} %bitcast.5, f32[56,64]{1,0:T(8,128)} %iw_ref.1, ...), custom_call_target="tpu_custom_call" | custom-call | tf_op jit(solution)/shard_map/indexer_grads/pallas_call | solution.py:525
  106.5 2.3 %hand_over.1 = (f32[3584,128]{1,0:T(8,128)}, f32[56,64]{1,0:T(8,128)}, f32[16,128]{1,0:T(8,128)}) custom-call(f32[3584,128]{1,0:T(8,128)} %get-tuple-element.9.gq_in, f32[56,64]{1,0:T(8,128)} %get-tuple-element.10.gw_in, f32[16,128]{1,0:T(8,128)} %get-tuple-element.11.gk_in), custom_call_target="tpu_custom_call" | custom-call | tf_op jit(solution)/shard_map/hand_over/pallas_call | solution.py:597
